TPU v7x, 32 devices: a whole 2x2x4 slice. The times are simulated.
32 devices in a mesh: req: 8 (over z, x), head: 4 (over y, core).
Axes of the slice: x: 2, y: 2, z: 4, core: 2. Of those that a mesh axis runs over, the one named last changes fastest.
Arguments:
- hidden_in: bfloat16 [8, 512, 2048], P('req', 'head'), may hold values from -16 to 16
- norm_gain: float32 [2048], replicated, may hold values from 0.1 to 1.9
- query_weight: bfloat16 [2048, 2048], P(None, 'head'), may hold values from -0.25 to 0.25
- key_weight: bfloat16 [2048, 512], P(None, 'head'), may hold values from -0.125 to 0.125
- value_weight: bfloat16 [2048, 512], P(None, 'head'), may hold values from -0.125 to 0.125
- output_weight: bfloat16 [2048, 2048], P('head'), may hold values from -0.75 to 0.75
- cache_keys: bfloat16 [8, 4096, 512], P('req', None, 'head'), may hold values from -256 to 256
- cache_values: bfloat16 [8, 4096, 512], P('req', None, 'head'), may hold values from -6 to 6
- held_states: bfloat16 [8, 384, 2048], P('req'), may hold values from -6 to 6
- cache_lengths: int32 [8], P('req'), may hold values from 512 to 4096, as said below
- recompute_index: int32 [8, 384], P('req'), may hold values from 0 to 4095, as said below
- slot_request: int32 [8], replicated, may hold values from 0 to 7, each once
Outputs:
- hidden_out: bfloat16 [8, 512, 2048], P('req', 'head')
- new_keys: bfloat16 [8, 512, 512], P('req', None, 'head')
- new_values: bfloat16 [8, 512, 512], P('req', None, 'head')
Inputs may be any that keep to these rules, and one draw needn't show every extreme that they name: `cache_lengths`: each slot's length; one slot holds exactly 4096 and one exactly 512. `recompute_index`: each slot's 384 entries are distinct positions below that slot's cache length. A permutation: slot s serves request slot_request[s].
All inputs are finite; a program needn't handle non-finite values.
Results may differ from a plain program's by a relative error of at most 0.018.
The roundings to bfloat16 on the way count: a program that leaves them out, or rounds other values in their place, can miss the bound.
Values may be sent and summed in bfloat16 or wider, within the bound.
No kernel may reach another device: no remote copies, remote signals or barrier semaphores. Data moves between devices by JAX's collectives and lax.ppermute only.
A program may use at most 64 MiB of HBM per device.

v0:
```python
import math

import jax
import jax.numpy as jnp
from jax import lax
from jax.sharding import PartitionSpec as P

H = 32
KVH = 8
HD = 64
KEY_BLOCK = 512


rope_base = 500000.0


def rms_scaled(matrix, gains):
    values = matrix.astype(jnp.float32)
    factor = lax.rsqrt(jnp.mean(values * values, axis=-1, keepdims=True) + 1e-05)
    return (values * factor * gains).astype(jnp.bfloat16)


def rotate(vectors, positions):
    halfway = vectors.shape[-1] // 2
    ladder = jnp.arange(halfway).astype(jnp.float32)
    frequency = jnp.exp(ladder * (-2.0 * math.log(rope_base) / vectors.shape[-1]))
    angles = positions[..., None, None] * frequency
    cosine = jnp.cos(angles)
    sine_part = jnp.sin(angles)
    former = vectors[..., :halfway]
    latter = vectors[..., halfway:]
    return jnp.concatenate(
        [former * cosine - latter * sine_part, latter * cosine + former * sine_part], axis=-1
    )


def route(blocks, ordering):
    requests_here, positions_here, features = blocks.shape
    groups = lax.axis_size("req")
    portion = positions_here // groups
    outgoing = blocks.reshape(requests_here, groups, portion, features)
    middle = lax.all_to_all(outgoing, "req", split_axis=1, concat_axis=1, tiled=True)
    flat_rows = middle.reshape(requests_here * groups, portion, features)
    wanted = jnp.transpose(ordering.reshape(groups, requests_here)).reshape(-1)
    source_row = wanted % requests_here * groups + wanted // requests_here
    picked = jnp.take(flat_rows, source_row, axis=0).reshape(
        requests_here, groups, portion, features
    )
    arrived = lax.all_to_all(picked, "req", split_axis=1, concat_axis=1, tiled=True)
    return arrived.reshape(requests_here, positions_here, features)


def shards(
    hidden_in,
    norm_gain,
    query_weight,
    key_weight,
    value_weight,
    output_weight,
    cache_keys,
    cache_values,
    held_states,
    cache_lengths,
    recompute_index,
    slot_request,
):
    requests_here, positions_here, features = hidden_in.shape
    total_new = positions_here * lax.axis_size("head")
    query_cols = query_weight.shape[1]
    key_cols = key_weight.shape[1]
    query_heads = query_cols // HD
    kv_heads = key_cols // HD
    per_group = H // KVH
    scaled = HD ** (-0.5)
    normed = rms_scaled(hidden_in, norm_gain)
    slotted = route(normed, slot_request)
    kv_joined = jnp.concatenate([key_weight, value_weight], axis=1)
    joined = jnp.concatenate([query_weight, kv_joined], axis=1)
    mixed = jnp.einsum(
        "rtd,de->rte",
        lax.all_gather(slotted, "head", axis=1, tiled=True),
        joined,
        preferred_element_type=jnp.float32,
    )
    spots = (
        cache_lengths.astype(jnp.float32)[:, None]
        + jnp.arange(total_new).astype(jnp.float32)[None, :]
    )
    queries = rotate(
        mixed[:, :, :query_cols].reshape(requests_here, total_new, query_heads, HD), spots
    ).astype(jnp.bfloat16)
    new_keys = (
        rotate(
            mixed[:, :, query_cols : query_cols + key_cols].reshape(
                requests_here, total_new, kv_heads, HD
            ),
            spots,
        )
        .astype(jnp.bfloat16)
        .reshape(requests_here, total_new, key_cols)
    )
    new_values = mixed[:, :, query_cols + key_cols :].astype(jnp.bfloat16)
    held_normed = rms_scaled(held_states, norm_gain)
    held_mix = jnp.einsum("rnd,de->rne", held_normed, kv_joined, preferred_element_type=jnp.float32)
    recompute_count = recompute_index.shape[1]
    held_keys = (
        rotate(
            held_mix[:, :, :key_cols].reshape(requests_here, recompute_count, kv_heads, HD),
            recompute_index.astype(jnp.float32),
        )
        .astype(jnp.bfloat16)
        .reshape(requests_here, recompute_count, key_cols)
    )
    held_values = held_mix[:, :, key_cols:].astype(jnp.bfloat16)
    place = jax.vmap(lambda initial, indices, fresh_rows: initial.at[indices].set(fresh_rows))
    keys_cache = place(cache_keys, recompute_index, held_keys).reshape(
        requests_here, -1, kv_heads, HD
    )
    values_cache = place(cache_values, recompute_index, held_values).reshape(
        requests_here, -1, kv_heads, HD
    )
    capacity = keys_cache.shape[1]
    grouped = queries.reshape(requests_here, total_new, kv_heads, per_group, HD)

    def accumulate(state, key_block, value_block, allowed):
        running_max, running_sum, running_acc = state
        scores = (
            jnp.einsum("rtcgd,rkcd->rcgtk", grouped, key_block, preferred_element_type=jnp.float32)
            * scaled
        )
        scores = jnp.where(allowed, scores, -1e30)
        new_max = jnp.maximum(running_max, jnp.max(scores, axis=-1))
        weights = jnp.where(allowed, jnp.exp(scores - new_max[..., None]), 0.0)
        shrink = jnp.exp(running_max - new_max)
        new_sum = running_sum * shrink + jnp.sum(weights, axis=-1)
        gathered = jnp.einsum(
            "rcgtk,rkcd->rtcgd",
            weights.astype(jnp.bfloat16),
            value_block,
            preferred_element_type=jnp.float32,
        )
        new_acc = running_acc * jnp.transpose(shrink, (0, 3, 1, 2))[..., None] + gathered
        return (new_max, new_sum, new_acc)

    start_state = (
        jnp.full((requests_here, kv_heads, per_group, total_new), -1e30, jnp.float32),
        jnp.zeros((requests_here, kv_heads, per_group, total_new), jnp.float32),
        jnp.zeros((requests_here, total_new, kv_heads, per_group, HD), jnp.float32),
    )
    causal = (jnp.arange(total_new)[None, :] <= jnp.arange(total_new)[:, None])[None, None, None]
    state = accumulate(
        start_state,
        new_keys.reshape(requests_here, total_new, kv_heads, HD),
        new_values.reshape(requests_here, total_new, kv_heads, HD),
        causal,
    )

    def visit(block_index, carried):
        offset = block_index * KEY_BLOCK
        key_block = lax.dynamic_slice_in_dim(keys_cache, offset, KEY_BLOCK, 1)
        value_block = lax.dynamic_slice_in_dim(values_cache, offset, KEY_BLOCK, 1)
        allowed = (offset + jnp.arange(KEY_BLOCK))[None, :] < cache_lengths[:, None]
        return accumulate(carried, key_block, value_block, allowed[:, None, None, None, :])

    block_count = capacity // KEY_BLOCK
    running_max, running_sum, running_acc = lax.fori_loop(0, block_count, visit, state)
    attended = (running_acc / jnp.transpose(running_sum, (0, 3, 1, 2))[..., None]).astype(
        jnp.bfloat16
    )
    attended = jnp.transpose(attended, (1, 0, 2, 3, 4)).reshape(
        total_new, requests_here, query_cols
    )
    summed = lax.psum_scatter(
        jnp.einsum(
            "tre,ed->trd", attended, output_weight, preferred_element_type=jnp.float32
        ).astype(jnp.bfloat16),
        "head",
        scatter_dimension=0,
        tiled=True,
    )
    projected = jnp.transpose(summed, (1, 0, 2))
    inverse = (
        jnp.zeros(slot_request.shape, jnp.int32)
        .at[slot_request]
        .set(jnp.arange(slot_request.shape[0], dtype=jnp.int32))
    )
    returned = route(projected, inverse)
    hidden_out = (hidden_in.astype(jnp.float32) + returned.astype(jnp.float32)).astype(jnp.bfloat16)
    return (hidden_out, new_keys, new_values)


def solution(mesh):
    return jax.shard_map(
        shards,
        mesh=mesh,
        in_specs=(
            P("req", "head", None),
            P(),
            P(None, "head"),
            P(None, "head"),
            P(None, "head"),
            P("head", None),
            P("req", None, "head"),
            P("req", None, "head"),
            P("req", None, None),
            P("req"),
            P("req", None),
            P(),
        ),
        out_specs=(P("req", "head", None), P("req", None, "head"), P("req", None, "head")),
        check_vma=False,
    )
```

profile of v0, /device:TPU:0, one launch (start us, length us, event | category | flops | bytes accessed | tf_op | source)
XLA Modules:
  0.0 256.4 jit_solution(9773656197976504830)
XLA Ops:
  7.2 2.4 copy.95
  10.9 2.0 fusion.66
  12.9 7.4 %all-to-all-start = ((bf16[1,8,16,2048]{3,2,0,1:T(8,128)(2,1)}), bf16[1,8,16,2048]{3,2,0,1:T(8,128)(2,1)}, u32[]{:S(2)}, u32[]{:S(2)}) async-start(bf16[1,8,16,2048]{3,2,0,1:T(8,128)(2,1)} %bitcast.233), calls=%async_computation | async-start | bytes 1048576 | tf_op jit(solution)/shard_map/all_to_all | solution.py:42
  21.7 13.2 %all-to-all-done = bf16[1,8,16,2048]{3,2,0,1:T(8,128)(2,1)} async-done(((bf16[1,8,16,2048]{3,2,0,1:T(8,128)(2,1)}), bf16[1,8,16,2048]{3,2,0,1:T(8,128)(2,1)}, u32[]{:S(2)}, u32[]{:S(2)}) %all-to-all-start) | async-done | bytes 524320 | tf_op jit(solution)/shard_map/all_to_all | solution.py:42
  34.9 2.4 gather_fusion
  38.5 18.2 %all_to_all.20 = bf16[1,8,16,2048]{3,2,0,1:T(8,128)(2,1)} all-to-all(bf16[1,8,16,2048]{3,2,0,1:T(8,128)(2,1)S(1)} %select_bitcast_fusion.1), channel_id=1, replica_groups=mesh['req'=8,'head'=4] {'req'}, dimensions={1} | all-to-all | bytes 1048576 | tf_op jit(solution)/shard_map/all_to_all | solution.py:49
  57.4 1.8 fusion.34
  59.2 2.5 fusion.61
  62.7 3.9 %scatter_fusion = bf16[4096,128]{1,0:T(8,128)(2,1)} fusion(bf16[4096,128]{1,0:T(8,128)(2,1)} %bitcast.225, s32[384]{0:T(512)S(1)} %fusion.79, bf16[384,128]{1,0:T(8,128)(2,1)S(1)} %copy.65), kind=kCustom, calls=%fused_computation.3 | custom fusion | bytes 296448 | tf_op jit(solution)/shard_map/vmap()/scatter | solution.py:115
  66.5 2.3 copy.66
  69.9 2.3 scatter_fusion.1
  74.0 4.5 %all-gather.2.cloned.1.call-done = bf16[1,512,2048]{2,1,0:T(8,128)(2,1)} async-done(((bf16[1,128,2048]{2,1,0:T(8,128)(2,1)}), bf16[1,512,2048]{2,1,0:T(8,128)(2,1)}) %all-gather.2.cloned.1.call-update) | async-done | bytes 2097168 | tf_op jit(solution)/shard_map/all_gather | solution.py:81
  78.5 4.3 %fusion.50 = f32[1,512,768]{2,1,0:T(8,128)S(1)} fusion(bf16[2048,128]{1,0:T(8,128)(2,1)} %param.20, bf16[2048,128]{1,0:T(8,128)(2,1)} %param.19, bf16[2048,512]{1,0:T(8,128)(2,1)} %param.18, bf16[1,512,2048]{2,1,0:T(8,128)(2,1)} %all-gather.2.cloned.1.call-done), kind=kOutput, calls=%fused_computation.63 | convolution fusion | flops 1620049920 | bytes 6815744 | tf_op jit(solution)/shard_map/rtd,de->rte/dot_general | solution.py:79
  89.8 3.2 %copy-done.1 = f32[2,512,512,4]{2,1,3,0:T(8,128)} copy-done((f32[2,512,512,4]{2,1,3,0:T(8,128)}, f32[2,512,512,4]{2,1,3,0:T(8,128)S(1)}, u32[]{:S(2)}) %copy-start.1) | copy-done | bytes 8388632
  92.9 2.0 fusion.29
  95.2 6.7 %fusion.58 = f32[1,512,2,4,64]{1,4,3,2,0:T(8,128)} fusion(bf16[512,2,64,1]{0,2,3,1:T(8,128)(2,1)S(1)} %bitcast.248, f32[2,512,512,4]{2,1,3,0:T(8,128)} %copy-done.1, f32[2,4,512]{2,1,0:T(4,128)S(1)} %get-tuple-element.205, pred[512,512]{0,1:T(8,128)(4,1)S(1)} %iota_compare_fusion, f32[512,2,4]{0,2,1:T(4,128)S(1)} %get-tuple-element.203), kind=kOutput, calls=%fused_computation.65 | convolution fusion | flops 279183360 | bytes 9863168 | tf_op jit(solution)/shard_map/rcgtk,rkcd->rtcgd/dot_general | solution.py:136
  101.9 69.4 %while.17 = (s32[]{:T(128)}, f32[1,2,4,512]{3,2,1,0:T(4,128)S(1)}, f32[1,2,4,512]{3,2,1,0:T(4,128)S(1)}, f32[1,512,2,4,64]{1,4,3,2,0:T(8,128)}, s32[1]{0:T(128)}...) while((s32[]{:T(128)}, f32[1,2,4,512]{3,2,1,0:T(4,128)S(1)}, ...), condition=%wide.region_9.11_spmd, body=%wide.region_6.10_spmd.sunk | while | flops 564671488 | bytes 36702952 | solution.py:166
  102.9 2.3 bitcast_reduce_fusion.2
  105.3 3.0 %fusion.102 = f32[1,512,2,4,64]{1,4,3,2,0:T(8,128)S(1)} fusion(f32[2,512,512,4]{2,1,3,0:T(8,128)S(1)} %get-tuple-element.268, f32[2,4,512]{2,1,0:T(4,128)S(1)} %bitcast.226, pred[512]{0:T(512)(128)(4,1)S(1)} %add_compare_fusion.2, f32[1,512,2,4,64]{1,4,3,2,0:T(8,128)S(1)} %copy-done.4, f32[512,2,4]{0,2,1:T(4,128)S(1)} %get-tuple-element.269, ...), kind=kOutput, calls=%fused_computation.17.clone.1 | convolution fusion | flops 279445504 | bytes 10650628 | tf_op jit(solution)/shard_map/while/body/eval_jaxpr/rcgtk,rkcd->rtcgd/dot_general | solution.py:136
  108.3 2.4 fusion.101
  111.6 2.3 bitcast_reduce_fusion.2
  113.9 3.0 %fusion.102 = f32[1,512,2,4,64]{1,4,3,2,0:T(8,128)S(1)} fusion(f32[2,512,512,4]{2,1,3,0:T(8,128)S(1)} %get-tuple-element.268, f32[2,4,512]{2,1,0:T(4,128)S(1)} %bitcast.226, pred[512]{0:T(512)(128)(4,1)S(1)} %add_compare_fusion.2, f32[1,512,2,4,64]{1,4,3,2,0:T(8,128)S(1)} %copy-done.4, f32[512,2,4]{0,2,1:T(4,128)S(1)} %get-tuple-element.269, ...), kind=kOutput, calls=%fused_computation.17.clone.1 | convolution fusion | flops 279445504 | bytes 10650628 | tf_op jit(solution)/shard_map/while/body/eval_jaxpr/rcgtk,rkcd->rtcgd/dot_general | solution.py:136
  117.0 2.4 fusion.101
  120.2 2.3 bitcast_reduce_fusion.2
  122.6 3.0 %fusion.102 = f32[1,512,2,4,64]{1,4,3,2,0:T(8,128)S(1)} fusion(f32[2,512,512,4]{2,1,3,0:T(8,128)S(1)} %get-tuple-element.268, f32[2,4,512]{2,1,0:T(4,128)S(1)} %bitcast.226, pred[512]{0:T(512)(128)(4,1)S(1)} %add_compare_fusion.2, f32[1,512,2,4,64]{1,4,3,2,0:T(8,128)S(1)} %copy-done.4, f32[512,2,4]{0,2,1:T(4,128)S(1)} %get-tuple-element.269, ...), kind=kOutput, calls=%fused_computation.17.clone.1 | convolution fusion | flops 279445504 | bytes 10650628 | tf_op jit(solution)/shard_map/while/body/eval_jaxpr/rcgtk,rkcd->rtcgd/dot_general | solution.py:136
  125.6 2.4 fusion.101
  128.9 2.3 bitcast_reduce_fusion.2
  131.2 3.0 %fusion.102 = f32[1,512,2,4,64]{1,4,3,2,0:T(8,128)S(1)} fusion(f32[2,512,512,4]{2,1,3,0:T(8,128)S(1)} %get-tuple-element.268, f32[2,4,512]{2,1,0:T(4,128)S(1)} %bitcast.226, pred[512]{0:T(512)(128)(4,1)S(1)} %add_compare_fusion.2, f32[1,512,2,4,64]{1,4,3,2,0:T(8,128)S(1)} %copy-done.4, f32[512,2,4]{0,2,1:T(4,128)S(1)} %get-tuple-element.269, ...), kind=kOutput, calls=%fused_computation.17.clone.1 | convolution fusion | flops 279445504 | bytes 10650628 | tf_op jit(solution)/shard_map/while/body/eval_jaxpr/rcgtk,rkcd->rtcgd/dot_general | solution.py:136
  134.3 2.4 fusion.101
  137.5 2.3 bitcast_reduce_fusion.2
  139.9 3.0 %fusion.102 = f32[1,512,2,4,64]{1,4,3,2,0:T(8,128)S(1)} fusion(f32[2,512,512,4]{2,1,3,0:T(8,128)S(1)} %get-tuple-element.268, f32[2,4,512]{2,1,0:T(4,128)S(1)} %bitcast.226, pred[512]{0:T(512)(128)(4,1)S(1)} %add_compare_fusion.2, f32[1,512,2,4,64]{1,4,3,2,0:T(8,128)S(1)} %copy-done.4, f32[512,2,4]{0,2,1:T(4,128)S(1)} %get-tuple-element.269, ...), kind=kOutput, calls=%fused_computation.17.clone.1 | convolution fusion | flops 279445504 | bytes 10650628 | tf_op jit(solution)/shard_map/while/body/eval_jaxpr/rcgtk,rkcd->rtcgd/dot_general | solution.py:136
  142.9 2.4 fusion.101
  146.2 2.3 bitcast_reduce_fusion.2
  148.5 3.0 %fusion.102 = f32[1,512,2,4,64]{1,4,3,2,0:T(8,128)S(1)} fusion(f32[2,512,512,4]{2,1,3,0:T(8,128)S(1)} %get-tuple-element.268, f32[2,4,512]{2,1,0:T(4,128)S(1)} %bitcast.226, pred[512]{0:T(512)(128)(4,1)S(1)} %add_compare_fusion.2, f32[1,512,2,4,64]{1,4,3,2,0:T(8,128)S(1)} %copy-done.4, f32[512,2,4]{0,2,1:T(4,128)S(1)} %get-tuple-element.269, ...), kind=kOutput, calls=%fused_computation.17.clone.1 | convolution fusion | flops 279445504 | bytes 10650628 | tf_op jit(solution)/shard_map/while/body/eval_jaxpr/rcgtk,rkcd->rtcgd/dot_general | solution.py:136
  151.6 2.4 fusion.101
  154.8 2.3 bitcast_reduce_fusion.2
  157.2 3.0 %fusion.102 = f32[1,512,2,4,64]{1,4,3,2,0:T(8,128)S(1)} fusion(f32[2,512,512,4]{2,1,3,0:T(8,128)S(1)} %get-tuple-element.268, f32[2,4,512]{2,1,0:T(4,128)S(1)} %bitcast.226, pred[512]{0:T(512)(128)(4,1)S(1)} %add_compare_fusion.2, f32[1,512,2,4,64]{1,4,3,2,0:T(8,128)S(1)} %copy-done.4, f32[512,2,4]{0,2,1:T(4,128)S(1)} %get-tuple-element.269, ...), kind=kOutput, calls=%fused_computation.17.clone.1 | convolution fusion | flops 279445504 | bytes 10650628 | tf_op jit(solution)/shard_map/while/body/eval_jaxpr/rcgtk,rkcd->rtcgd/dot_general | solution.py:136
  160.2 2.4 fusion.101
  163.5 2.3 bitcast_reduce_fusion.2
  165.8 3.0 %fusion.102 = f32[1,512,2,4,64]{1,4,3,2,0:T(8,128)S(1)} fusion(f32[2,512,512,4]{2,1,3,0:T(8,128)S(1)} %get-tuple-element.268, f32[2,4,512]{2,1,0:T(4,128)S(1)} %bitcast.226, pred[512]{0:T(512)(128)(4,1)S(1)} %add_compare_fusion.2, f32[1,512,2,4,64]{1,4,3,2,0:T(8,128)S(1)} %copy-done.4, f32[512,2,4]{0,2,1:T(4,128)S(1)} %get-tuple-element.269, ...), kind=kOutput, calls=%fused_computation.17.clone.1 | convolution fusion | flops 279445504 | bytes 10650628 | tf_op jit(solution)/shard_map/while/body/eval_jaxpr/rcgtk,rkcd->rtcgd/dot_general | solution.py:136
  168.8 2.4 fusion.101
  172.8 2.6 %fusion.43 = bf16[512,1,2048]{2,0,1:T(8,128)(2,1)} fusion(bf16[512,512]{0,1:T(8,128)(2,1)S(1)} %bitcast.242, bf16[512,2048]{1,0:T(8,128)(2,1)S(1)} %copy-done), kind=kOutput, calls=%fused_computation.54 | convolution fusion | flops 1074790400 | bytes 4718592 | tf_op jit(solution)/shard_map/tre,ed->trd/dot_general | solution.py:174
  175.4 31.6 %reduce-scatter.2.cloned.1.call-done = bf16[128,1,2048]{2,0,1:T(8,128)(2,1)} async-done(((bf16[512,1,2048]{2,0,1:T(8,128)(2,1)}), bf16[128,1,2048]{2,0,1:T(8,128)(2,1)}) %reduce-scatter.2.cloned.1.call-update) | async-done | bytes 524304 | tf_op jit(solution)/shard_map/reduce_scatter | solution.py:173
  207.0 5.5 %all-to-all-start.2 = ((bf16[1,8,16,2048]{3,2,0,1:T(8,128)(2,1)}), bf16[1,8,16,2048]{3,2,0,1:T(8,128)(2,1)S(1)}, u32[]{:S(2)}, u32[]{:S(2)}) async-start(bf16[1,8,16,2048]{3,2,0,1:T(8,128)(2,1)} %bitcast.243), calls=%async_computation.3 | async-start | bytes 1048576 | tf_op jit(solution)/shard_map/all_to_all | solution.py:42
  213.2 13.8 %all-to-all-done.2 = bf16[1,8,16,2048]{3,2,0,1:T(8,128)(2,1)S(1)} async-done(((bf16[1,8,16,2048]{3,2,0,1:T(8,128)(2,1)}), bf16[1,8,16,2048]{3,2,0,1:T(8,128)(2,1)S(1)}, u32[]{:S(2)}, u32[]{:S(2)}) %all-to-all-start.2) | async-done | bytes 524320 | tf_op jit(solution)/shard_map/all_to_all | solution.py:42
  228.4 1.9 select_bitcast_fusion
  230.4 3.6 %all-to-all-start.3 = ((bf16[1,8,16,2048]{3,2,0,1:T(8,128)(2,1)}), bf16[1,8,16,2048]{3,2,0,1:T(8,128)(2,1)S(1)}, u32[]{:S(2)}, u32[]{:S(2)}) async-start(bf16[1,8,16,2048]{3,2,0,1:T(8,128)(2,1)} %select_bitcast_fusion), calls=%async_computation.4 | async-start | bytes 1048576 | tf_op jit(solution)/shard_map/all_to_all | solution.py:49
  234.8 13.9 %all-to-all-done.3 = bf16[1,8,16,2048]{3,2,0,1:T(8,128)(2,1)S(1)} async-done(((bf16[1,8,16,2048]{3,2,0,1:T(8,128)(2,1)}), bf16[1,8,16,2048]{3,2,0,1:T(8,128)(2,1)S(1)}, u32[]{:S(2)}, u32[]{:S(2)}) %all-to-all-start.3) | async-done | bytes 524320 | tf_op jit(solution)/shard_map/all_to_all | solution.py:49
  (140 shorter events, 25.9 us)
Async XLA Ops:
  7.2 165.6 %copy-start = (bf16[512,2048]{1,0:T(8,128)(2,1)S(1)}, bf16[512,2048]{1,0:T(8,128)(2,1)}, u32[]{:S(2)}) copy-start(bf16[512,2048]{1,0:T(8,128)(2,1)} %param.21) | copy-start | bytes 6291460
  7.2 52.0 %copy-start.14 = (f32[2048]{0:T(1024)S(1)}, f32[2048]{0:T(1024)}, u32[]{:S(2)}) copy-start(f32[2048]{0:T(1024)} %param.17) | copy-start | bytes 24580
  7.2 54.6 %copy-start.15 = (s32[1,384]{1,0:T(1,128)S(1)}, s32[1,384]{1,0:T(1,128)}, u32[]{:S(2)}) copy-start(s32[1,384]{1,0:T(1,128)} %param.26) | copy-start | bytes 4612
  12.9 57.0 %copy-start.2 = (bf16[1,4096,128]{2,1,0:T(8,128)(2,1)S(1)}, bf16[1,4096,128]{2,1,0:T(8,128)(2,1)}, u32[]{:S(2)}) copy-start(bf16[1,4096,128]{2,1,0:T(8,128)(2,1)} %param.23) | copy-start | bytes 3145732
  12.9 22.0 %all-to-all-start = ((bf16[1,8,16,2048]{3,2,0,1:T(8,128)(2,1)}), bf16[1,8,16,2048]{3,2,0,1:T(8,128)(2,1)}, u32[]{:S(2)}, u32[]{:S(2)}) async-start(bf16[1,8,16,2048]{3,2,0,1:T(8,128)(2,1)} %bitcast.233), calls=%async_computation | async-start | bytes 1048576 | tf_op jit(solution)/shard_map/all_to_all | solution.py:42
  20.3 58.2 %all-gather.2.cloned.1.call-start = ((), (), s32[]{:S(2)}) async-start(), calls=%async_computation.5 | async-start | bytes 2621440 | tf_op jit(solution)/shard_map/all_gather | solution.py:81
  56.7 150.3 %reduce-scatter.2.cloned.1.call-start = ((), (), s32[]{:S(2)}) async-start(), calls=%async_computation.6 | async-start | bytes 2621440 | tf_op jit(solution)/shard_map/reduce_scatter | solution.py:173
  61.7 0.7 copy-start.13
  88.2 6.8 %copy-start.6 = (bf16[1,512,8,32]{1,3,2,0:T(8,128)(2,1)}, bf16[1,512,8,32]{1,3,2,0:T(8,128)(2,1)S(1)}, u32[]{:S(2)}) copy-start(bf16[1,512,8,32]{1,3,2,0:T(8,128)(2,1)S(1)} %get-tuple-element.198) | copy-start | bytes 786436
  88.2 1.5 copy-start.9
  88.2 6.7 %copy-start.11 = (bf16[1,512,2,32]{1,3,2,0:T(8,128)(2,1)}, bf16[1,512,2,32]{1,3,2,0:T(8,128)(2,1)S(1)}, u32[]{:S(2)}) copy-start(bf16[1,512,2,32]{1,3,2,0:T(8,128)(2,1)S(1)} %get-tuple-element.200) | copy-start | bytes 196612
  88.3 6.8 %copy-start.8 = (bf16[1,512,128]{2,1,0:T(8,128)(2,1)S(1)}, bf16[1,512,128]{2,1,0:T(8,128)(2,1)}, u32[]{:S(2)}) copy-start(bf16[1,512,128]{2,1,0:T(8,128)(2,1)} %slice.85) | copy-start | bytes 393220
  89.7 3.2 %copy-start.1 = (f32[2,512,512,4]{2,1,3,0:T(8,128)}, f32[2,512,512,4]{2,1,3,0:T(8,128)S(1)}, u32[]{:S(2)}) copy-start(f32[2,512,512,4]{2,1,3,0:T(8,128)S(1)} %get-tuple-element.212) | copy-start | bytes 25165828
  95.2 6.7 %copy-start.7 = (bf16[1,512,8,32]{1,3,2,0:T(8,128)(2,1)S(1)}, bf16[1,512,8,32]{1,3,2,0:T(8,128)(2,1)}, u32[]{:S(2)}) copy-start(bf16[1,512,8,32]{1,3,2,0:T(8,128)(2,1)} %copy-done.6) | copy-start | bytes 786436
  102.2 3.1 %copy-start.4 = (f32[1,512,2,4,64]{1,4,3,2,0:T(8,128)S(1)}, f32[1,512,2,4,64]{1,4,3,2,0:T(8,128)}, u32[]{:S(2)}) copy-start(f32[1,512,2,4,64]{1,4,3,2,0:T(8,128)} %get-tuple-element.285) | copy-start | bytes 3145732 | tf_op jit(solution)/shard_map/while
  108.3 2.5 copy-start.5
  110.8 3.1 %copy-start.4 = (f32[1,512,2,4,64]{1,4,3,2,0:T(8,128)S(1)}, f32[1,512,2,4,64]{1,4,3,2,0:T(8,128)}, u32[]{:S(2)}) copy-start(f32[1,512,2,4,64]{1,4,3,2,0:T(8,128)} %get-tuple-element.285) | copy-start | bytes 3145732 | tf_op jit(solution)/shard_map/while
  117.0 2.5 copy-start.5
  119.5 3.1 %copy-start.4 = (f32[1,512,2,4,64]{1,4,3,2,0:T(8,128)S(1)}, f32[1,512,2,4,64]{1,4,3,2,0:T(8,128)}, u32[]{:S(2)}) copy-start(f32[1,512,2,4,64]{1,4,3,2,0:T(8,128)} %get-tuple-element.285) | copy-start | bytes 3145732 | tf_op jit(solution)/shard_map/while
  125.6 2.5 copy-start.5
  128.1 3.1 %copy-start.4 = (f32[1,512,2,4,64]{1,4,3,2,0:T(8,128)S(1)}, f32[1,512,2,4,64]{1,4,3,2,0:T(8,128)}, u32[]{:S(2)}) copy-start(f32[1,512,2,4,64]{1,4,3,2,0:T(8,128)} %get-tuple-element.285) | copy-start | bytes 3145732 | tf_op jit(solution)/shard_map/while
  134.3 2.5 copy-start.5
  136.8 3.1 %copy-start.4 = (f32[1,512,2,4,64]{1,4,3,2,0:T(8,128)S(1)}, f32[1,512,2,4,64]{1,4,3,2,0:T(8,128)}, u32[]{:S(2)}) copy-start(f32[1,512,2,4,64]{1,4,3,2,0:T(8,128)} %get-tuple-element.285) | copy-start | bytes 3145732 | tf_op jit(solution)/shard_map/while
  142.9 2.5 copy-start.5
  145.4 3.1 %copy-start.4 = (f32[1,512,2,4,64]{1,4,3,2,0:T(8,128)S(1)}, f32[1,512,2,4,64]{1,4,3,2,0:T(8,128)}, u32[]{:S(2)}) copy-start(f32[1,512,2,4,64]{1,4,3,2,0:T(8,128)} %get-tuple-element.285) | copy-start | bytes 3145732 | tf_op jit(solution)/shard_map/while
  151.5 2.5 copy-start.5
  154.1 3.1 %copy-start.4 = (f32[1,512,2,4,64]{1,4,3,2,0:T(8,128)S(1)}, f32[1,512,2,4,64]{1,4,3,2,0:T(8,128)}, u32[]{:S(2)}) copy-start(f32[1,512,2,4,64]{1,4,3,2,0:T(8,128)} %get-tuple-element.285) | copy-start | bytes 3145732 | tf_op jit(solution)/shard_map/while
  160.2 2.5 copy-start.5
  162.7 3.1 %copy-start.4 = (f32[1,512,2,4,64]{1,4,3,2,0:T(8,128)S(1)}, f32[1,512,2,4,64]{1,4,3,2,0:T(8,128)}, u32[]{:S(2)}) copy-start(f32[1,512,2,4,64]{1,4,3,2,0:T(8,128)} %get-tuple-element.285) | copy-start | bytes 3145732 | tf_op jit(solution)/shard_map/while
  168.8 2.5 copy-start.5
  171.3 62.7 %copy-start.10 = (bf16[1,512,2,32]{1,3,2,0:T(8,128)(2,1)S(1)}, bf16[1,512,2,32]{1,3,2,0:T(8,128)(2,1)}, u32[]{:S(2)}) copy-start(bf16[1,512,2,32]{1,3,2,0:T(8,128)(2,1)} %copy-done.9) | copy-start | bytes 196612
  171.3 62.7 %copy-start.12 = (bf16[1,512,2,32]{1,3,2,0:T(8,128)(2,1)S(1)}, bf16[1,512,2,32]{1,3,2,0:T(8,128)(2,1)}, u32[]{:S(2)}) copy-start(bf16[1,512,2,32]{1,3,2,0:T(8,128)(2,1)} %copy-done.11) | copy-start | bytes 196612
  171.4 77.3 %copy-start.3 = (bf16[1,128,2048]{2,1,0:T(8,128)(2,1)S(1)}, bf16[1,128,2048]{2,1,0:T(8,128)(2,1)}, u32[]{:S(2)}) copy-start(bf16[1,128,2048]{2,1,0:T(8,128)(2,1)} %param.16) | copy-start | bytes 1572868
  207.0 20.0 %all-to-all-start.2 = ((bf16[1,8,16,2048]{3,2,0,1:T(8,128)(2,1)}), bf16[1,8,16,2048]{3,2,0,1:T(8,128)(2,1)S(1)}, u32[]{:S(2)}, u32[]{:S(2)}) async-start(bf16[1,8,16,2048]{3,2,0,1:T(8,128)(2,1)} %bitcast.243), calls=%async_computation.3 | async-start | bytes 1048576 | tf_op jit(solution)/shard_map/all_to_all | solution.py:42
  230.4 18.3 %all-to-all-start.3 = ((bf16[1,8,16,2048]{3,2,0,1:T(8,128)(2,1)}), bf16[1,8,16,2048]{3,2,0,1:T(8,128)(2,1)S(1)}, u32[]{:S(2)}, u32[]{:S(2)}) async-start(bf16[1,8,16,2048]{3,2,0,1:T(8,128)(2,1)} %select_bitcast_fusion), calls=%async_computation.4 | async-start | bytes 1048576 | tf_op jit(solution)/shard_map/all_to_all | solution.py:49
Sparse Core Ops, SparseCore 0:
  56.8 21.6 all-gather.1
  175.6 31.4 reduce-scatter.1
where the time goes:
time: 258 us; the launch traced here: 256 us
  waiting for transfers between devices  77.1 us (30%)
  matrix products  60.3 us (23%)
  other arithmetic  41.8 us (16%)
  local copies, waits for them, and re-layouts  26.4 us (10%)
  blocking collectives  18.2 us (7%)
  starting transfers between devices  16.6 us (6%)
  between operations  15.1 us (6%)
    reduce_scatter x1, waiting for transfers between devices, shards(): lax.psum_scatter(jnp.einsum('tre,ed->trd', attended, output_weight, prefe...  31.6 us
    dot_general x9, matrix products, accumulate(): jnp.einsum('rcgtk,rkcd->rtcgd', weights.astype(jnp.bfloat16), value_block...  30.8 us
    all_to_all x2, waiting for transfers between devices, route(): lax.all_to_all(outgoing, 'req', split_axis=1, concat_axis=1, tiled=True)  27.1 us
    reduce_sum x9, other arithmetic, accumulate(): new_sum = running_sum * shrink + jnp.sum(weights, axis=-1)  21.5 us
    dot_general x9, matrix products, accumulate(): jnp.einsum('rtcgd,rkcd->rcgtk', grouped, key_block, preferred_element_typ...  20 us
    all_to_all x1, blocking collectives, route(): lax.all_to_all(picked, 'req', split_axis=1, concat_axis=1, tiled=True)  18.2 us
    all_to_all x1, waiting for transfers between devices, route(): lax.all_to_all(picked, 'req', split_axis=1, concat_axis=1, tiled=True)  13.9 us
    all_to_all x2, starting transfers between devices, route(): lax.all_to_all(outgoing, 'req', split_axis=1, concat_axis=1, tiled=True)  12.9 us
  transfers between devices with their start and end apart: 5, of which 5 were waited for; matrix products, arithmetic and copies ran while one was open for 7% of the time, Pallas kernels for 0%

commit v1 on v0

v1 whole, which is shorter than its diff:
```python
import functools, math
import jax
import jax.numpy as jnp
from jax import lax
from jax.experimental import pallas as pl
from jax.experimental.pallas import tpu as pltpu
from jax.sharding import PartitionSpec as P

HD = 64
LANES = 128
F32 = jnp.float32
BF16 = jnp.bfloat16
ROPE_BASE = 500000.0
MASKED = -1e30
TOP = 2.0**100
FACTOR = HD**-0.5 * math.log2(math.e)
NT = (((1,), (1,)), ((), ()))
VM = pl.BlockSpec(memory_space=pltpu.VMEM)
SM = pl.BlockSpec(memory_space=pltpu.SMEM)


def rms_scaled(values, gains):
    factor = lax.rsqrt(jnp.mean(values * values, axis=-1, keepdims=True) + 1e-05)
    return (values * factor * gains).astype(BF16)


def lane_of(shape):
    return lax.broadcasted_iota(jnp.int32, shape, len(shape) - 1)


def turned(x, cosine, sine):
    lane = lane_of(x.shape)
    swapped = jnp.where(
        lane % HD < HD // 2, pltpu.roll(x, LANES - HD // 2, 1), pltpu.roll(x, HD // 2, 1)
    )
    return x * cosine + swapped * sine


def head_lanes(x, which):
    return x if which == 0 else pltpu.roll(x, HD, 1)


def key_rows(k, which, bias):
    lane = lane_of(k.shape)
    tail = jnp.where(lane == HD, 1.0, jnp.where(lane == HD + 1, bias, 0.0))
    return jnp.where(lane < HD, head_lanes(k, which), tail).astype(BF16)


def value_rows(v, which):
    lane = lane_of(v.shape)
    return jnp.where(lane < HD, head_lanes(v, which), jnp.where(lane == HD, 1.0, 0.0)).astype(BF16)


def prep_kernel(length, held, gain, wk, wv, cosine, sine, index, ck, cv, ka, va, fresh):
    normed = rms_scaled(held[...].astype(F32), gain[...])
    k = jnp.dot(normed, wk[...], preferred_element_type=F32)
    fresh[:, :LANES] = turned(k, cosine[...], sine[...]).astype(BF16)
    fresh[:, LANES:] = jnp.dot(normed, wv[...], preferred_element_type=F32).astype(BF16)
    step = 512
    count = held.shape[0]

    def body(b, _):
        base = pl.multiple_of(b * step, step)
        rows = lax.broadcasted_iota(jnp.int32, (step, count), 0) + base
        hit = (rows == index[...]).astype(F32)
        placed = jnp.dot(hit.astype(BF16), fresh[...], preferred_element_type=F32)
        taken = jnp.max(hit, axis=1, keepdims=True) > 0.0
        at = pl.ds(base, step)
        kk = jnp.where(taken, placed[:, :LANES], ck[at, :].astype(F32))
        vv = jnp.where(taken, placed[:, LANES:], cv[at, :].astype(F32))
        row = lax.broadcasted_iota(jnp.int32, (step, LANES), 0) + base
        bias = jnp.where(row < length[0], 0.0, MASKED)
        for j in range(2):
            ka[j, at, :] = key_rows(kk, j, bias)
            va[j, at, :] = value_rows(vv, j)
        return 0

    lax.fori_loop(0, ck.shape[0] // step, body, 0)


def prep(length, held, gain, wk, wv, cosine, sine, index, ck, cv):
    cap = ck.shape[0]
    out = jax.ShapeDtypeStruct((2, cap, LANES), BF16)
    return pl.pallas_call(
        prep_kernel,
        out_shape=(out, out),
        in_specs=[SM] + [VM] * 9,
        out_specs=(VM, VM),
        scratch_shapes=[pltpu.VMEM((held.shape[0], 2 * LANES), BF16)],
        compiler_params=pltpu.CompilerParams(vmem_limit_bytes=40 << 20),
        cost_estimate=pl.CostEstimate(flops=3 * 10**9, bytes_accessed=8 << 20, transcendentals=0),
        name="prep",
    )(length, held, gain, wk, wv, cosine, sine, index, ck, cv)


def qkv_kernel(pieces, *refs):
    xs, (wq, wk, wv, cosine, sine, q, k, v, x) = refs[:pieces], refs[pieces:]
    rows = xs[0].shape[0]
    for i, piece in enumerate(xs):
        x[i * rows : (i + 1) * rows, :] = piece[...]
    c, s = cosine[...], sine[...]
    xv = x[...]
    for j in range(wq.shape[1] // 256):
        got = jnp.dot(xv, wq[:, j * 256 : (j + 1) * 256], preferred_element_type=F32)
        for t in range(2):
            at = slice(j * 256 + t * LANES, j * 256 + (t + 1) * LANES)
            q[:, at] = turned(got[:, t * LANES : (t + 1) * LANES], c, s).astype(BF16)
    k[...] = turned(jnp.dot(xv, wk[...], preferred_element_type=F32), c, s).astype(BF16)
    v[...] = jnp.dot(xv, wv[...], preferred_element_type=F32).astype(BF16)


def qkv(xs, wq, wk, wv, cosine, sine):
    rows = sum(x.shape[0] for x in xs)
    out = lambda n: jax.ShapeDtypeStruct((rows, n), BF16)
    return pl.pallas_call(
        functools.partial(qkv_kernel, len(xs)),
        out_shape=(out(wq.shape[1]), out(LANES), out(LANES)),
        in_specs=[VM] * (len(xs) + 5),
        out_specs=(VM,) * 3,
        scratch_shapes=[pltpu.VMEM((rows, xs[0].shape[1]), BF16)],
        compiler_params=pltpu.CompilerParams(vmem_limit_bytes=24 << 20),
        cost_estimate=pl.CostEstimate(
            flops=2 * rows * 2048 * 768, bytes_accessed=5 << 20, transcendentals=0
        ),
        name="qkv",
    )(*xs, wq, wk, wv, cosine, sine)


KEYS = 512
CHUNKS = 1


def att_kernel(portion, chunk, chunks, scal, q, ka, va, *refs):
    kn, vn = refs[:chunks], refs[chunks : 2 * chunks]
    o, qa, na, nv, acc, low = refs[2 * chunks :]
    tokens = q.shape[0]
    length, head = scal[0], scal[1]
    per = q.shape[1] // HD // 2
    rows = per * tokens
    blocks = lax.div(length + (KEYS - 1), KEYS)

    def token(i, part):
        which = lax.div(i, portion)
        return (which ^ head) * (portion * chunks) + part * portion + (i - which * portion)

    own = token(lax.broadcasted_iota(jnp.int32, (tokens, tokens), 0), chunk)
    allowed = [
        token(lax.broadcasted_iota(jnp.int32, (tokens, tokens), 1), part) <= own
        for part in range(chunks)
    ]
    lane = lane_of((tokens, LANES))
    for j in range(2):
        for part in range(chunks):
            na[part] = key_rows(kn[part][...].astype(F32), j, 0.0)
            nv[part] = value_rows(vn[part][...].astype(F32), j)

        def put_queries(g, offset):
            pair = (j * per + g) // 2
            x = q[:, pair * LANES : (pair + 1) * LANES].astype(F32)
            tail = jnp.where(lane == HD, offset, jnp.where(lane == HD + 1, 1.0, 0.0))
            qa[g * tokens : (g + 1) * tokens, :] = jnp.where(
                lane < HD, head_lanes(x, g % 2), tail
            ).astype(BF16)

        for g in range(per):
            put_queries(g, 0.0)
            at = slice(g * tokens, (g + 1) * tokens)
            first = lax.dot_general(qa[at, :], ka[j, :256, :], NT, preferred_element_type=F32)
            put_queries(g, -jnp.max(first, axis=1, keepdims=True))

        def weights(keys, at):
            s = lax.dot_general(qa[at, :], keys, NT, preferred_element_type=F32)
            return jnp.exp2(s * FACTOR)

        for g in range(per):
            at = slice(g * tokens, (g + 1) * tokens)
            total = jnp.zeros((tokens, LANES), F32)
            for part in range(chunks):
                p = jnp.where(allowed[part], weights(na[part], at), 0.0)
                total += jnp.dot(p.astype(BF16), nv[part], preferred_element_type=F32)
            acc[at, :] = total

        def body(b, _):
            at = pl.ds(pl.multiple_of(b * KEYS, KEYS), KEYS)
            keys, values = ka[j, at, :], va[j, at, :]
            for g in range(per):
                q_at = slice(g * tokens, (g + 1) * tokens)
                p = weights(keys, q_at).astype(BF16)
                acc[q_at, :] += jnp.dot(p, values, preferred_element_type=F32)
            return 0

        lax.fori_loop(0, blocks, body, 0)

        safe = jnp.min((acc[:, HD : HD + 1] < TOP).astype(F32)) > 0.5

        @pl.when(jnp.logical_not(safe))
        def _():
            for g in range(per):
                put_queries(g, 0.0)
            acc[...] = jnp.zeros_like(acc)
            low[...] = jnp.full_like(low, MASKED)

            def take(keys, values, permitted, at):
                s = lax.dot_general(qa[at, :], keys, NT, preferred_element_type=F32)
                if permitted is not None:
                    s = jnp.where(permitted, s, MASKED)
                past = low[at, :]
                top = jnp.maximum(past, jnp.max(s, axis=1, keepdims=True))
                p = jnp.exp2((s - top[:, :1]) * FACTOR)
                shrink = jnp.exp2((past - top) * FACTOR)
                low[at, :] = top
                acc[at, :] = acc[at, :] * shrink + jnp.dot(
                    p.astype(BF16), values, preferred_element_type=F32
                )

            def redo(b, _):
                at = pl.ds(pl.multiple_of(b * KEYS, KEYS), KEYS)
                for g in range(per):
                    take(ka[j, at, :], va[j, at, :], None, slice(g * tokens, (g + 1) * tokens))
                return 0

            lax.fori_loop(0, blocks, redo, 0)
            for g in range(per):
                for part in range(chunks):
                    take(na[part], nv[part], allowed[part], slice(g * tokens, (g + 1) * tokens))

        for g in range(0, per, 2):
            pair = []
            for t in range(2):
                got = acc[(g + t) * tokens : (g + t + 1) * tokens, :]
                pair.append(got / got[:, HD : HD + 1])
            at = slice((j * per + g) * HD, (j * per + g + 2) * HD)
            o[:, at] = jnp.where(lane < HD, pair[0], pltpu.roll(pair[1], HD, 1)).astype(BF16)


def attend(portion, chunk, scal, q, ka, va, kns, vns):
    tokens, chunks = q.shape[0], len(kns)
    rows = q.shape[1] // HD // 2 * tokens
    return pl.pallas_call(
        functools.partial(att_kernel, portion, chunk, chunks),
        out_shape=jax.ShapeDtypeStruct(q.shape, BF16),
        in_specs=[SM] + [VM] * (3 + 2 * chunks),
        out_specs=VM,
        scratch_shapes=[
            pltpu.VMEM((rows, LANES), BF16),
            pltpu.VMEM((chunks, tokens, LANES), BF16),
            pltpu.VMEM((chunks, tokens, LANES), BF16),
            pltpu.VMEM((rows, LANES), F32),
            pltpu.VMEM((rows, LANES), F32),
        ],
        compiler_params=pltpu.CompilerParams(vmem_limit_bytes=40 << 20),
        cost_estimate=pl.CostEstimate(
            flops=4 * rows * 2 * 4608 * 128, bytes_accessed=6 << 20, transcendentals=rows * 2 * 4608
        ),
        name="attend",
    )(scal, q, ka, va, *kns, *vns)


def tables(positions):
    ladder = jnp.arange(HD // 2).astype(F32)
    frequency = jnp.exp(ladder * (-2.0 * math.log(ROPE_BASE) / HD))
    angles = positions[:, None] * frequency
    cosine, sine = jnp.cos(angles), jnp.sin(angles)
    return (
        jnp.concatenate([cosine] * 4, axis=-1),
        jnp.concatenate([-sine, sine, -sine, sine], axis=-1),
    )


def pick_kernel(order, x, out):
    for s in range(out.shape[0]):
        out[s] = x[order[s]]


def pick(x, order):
    return pl.pallas_call(
        pick_kernel,
        out_shape=jax.ShapeDtypeStruct(x.shape, x.dtype),
        in_specs=[SM, VM],
        out_specs=VM,
        name="pick",
    )(order, x)


def swap(x, axis, bits):
    size = lax.axis_size(axis)
    return lax.ppermute(x, axis, [(i, i ^ bits) for i in range(size)])


def spread(x):
    groups = lax.axis_size("req")
    rows, features = x.shape
    pieces = x.reshape(groups, rows // groups, features)
    return lax.all_to_all(pieces, "req", split_axis=0, concat_axis=0, tiled=True)


def shards(
    hidden_in,
    norm_gain,
    query_weight,
    key_weight,
    value_weight,
    output_weight,
    cache_keys,
    cache_values,
    held_states,
    cache_lengths,
    recompute_index,
    slot_request,
):
    requests_here, positions_here, features = hidden_in.shape
    assert requests_here == 1
    heads = lax.axis_size("head")
    head = lax.axis_index("head")
    portion = positions_here // CHUNKS
    mine = hidden_in[0]
    gain = norm_gain[None, :]
    normed = rms_scaled(mine.astype(F32), gain)
    length = cache_lengths[0]
    relative = jnp.arange(heads) ^ head
    tables_of = [
        tables(
            (
                relative[:, None] * positions_here + part * portion + jnp.arange(portion)[None, :]
            ).reshape(-1).astype(F32)
            + length.astype(F32)
        )
        for part in range(CHUNKS)
    ]
    scal = jnp.stack([length, head.astype(jnp.int32)])

    parts = [normed[c * portion : (c + 1) * portion] for c in range(CHUNKS)]
    spreads = [spread(x) for x in parts]
    slotted = [spread(pick(x, slot_request).reshape(portion, features)) for x in spreads]

    held_cos, held_sin = tables(recompute_index[0].astype(F32))
    ka, va = prep(
        cache_lengths,
        held_states[0],
        gain,
        key_weight,
        value_weight,
        held_cos,
        held_sin,
        recompute_index,
        cache_keys[0],
        cache_values[0],
    )

    qs, kns, vns = [], [], []
    for c in range(CHUNKS):
        own = slotted[c].reshape(portion, features)
        order = {0: own}
        step = heads // 2
        while step >= 1:
            for d in list(order):
                order[d | step] = swap(order[d], "head", step)
            step //= 2
        xs = [order[d] for d in range(heads)]
        q, kn, vn = qkv(xs, query_weight, key_weight, value_weight, *tables_of[c])
        qs.append(q)
        kns.append(kn)
        vns.append(vn)

    slots = jnp.arange(slot_request.shape[0], dtype=jnp.int32)
    inverse = jnp.sum(jnp.where(slot_request[None, :] == slots[:, None], slots[None, :], 0), axis=1)
    backs = []
    for c in range(CHUNKS):
        attended = attend(portion, c, scal, qs[c], ka, va, kns, vns)
        terms = jnp.dot(attended, output_weight, preferred_element_type=F32).astype(BF16)
        terms = terms.reshape(heads, portion, features)
        total = terms[0].astype(F32)
        for d in range(1, heads):
            total = total + swap(terms[d], "head", d).astype(F32)
        backs.append(spread(total.astype(BF16)))
    returned = [spread(pick(x, inverse).reshape(portion, features)) for x in backs]
    returned = jnp.concatenate([x.reshape(portion, features) for x in returned], axis=0)
    hidden_out = (mine.astype(F32) + returned.astype(F32)).astype(BF16)

    def by_token(pieces):
        stacked = jnp.stack([x.reshape(heads, portion, LANES) for x in pieces], axis=1)
        return jnp.take(stacked, relative, axis=0).reshape(1, heads * positions_here, LANES)

    return (hidden_out[None], by_token(kns), by_token(vns))


def solution(mesh):
    return jax.shard_map(
        shards,
        mesh=mesh,
        in_specs=(
            P("req", "head", None),
            P(),
            P(None, "head"),
            P(None, "head"),
            P(None, "head"),
            P("head", None),
            P("req", None, "head"),
            P("req", None, "head"),
            P("req", None, None),
            P("req"),
            P("req", None),
            P(),
        ),
        out_specs=(P("req", "head", None), P("req", None, "head"), P("req", None, "head")),
        check_vma=False,
    )
```

time: 258 us -> 210 us (0.81)
  matrix products: 60.3 us -> 1.29 us
  Pallas kernels: 0 us -> 47.3 us
  starting transfers between devices: 16.6 us -> 53.3 us
  other arithmetic: 41.8 us -> 8.92 us
  local copies, waits for them, and re-layouts: 26.4 us -> 3.26 us
  between operations: 15.1 us -> 1.53 us
  waiting for transfers between devices: 77.1 us -> 72.3 us
  blocking collectives: 18.2 us -> 21.7 us
    dot_general x21 -> x1, matrix products: 60.3 us -> 1.29 us  [shards(): jnp.dot(attended, output_weight, preferred_element_type=F32).astype(BF16)]
    pallas_call x0 -> x5, Pallas kernels: none -> 47.3 us  [the longest x1 36.5 us: attend(): pl.pallas_call(functools.partial(att_kernel, portion, chunk, chunks), out...]
    all_to_all x3, starting transfers between devices: 16.5 us -> 49.6 us  [spread(): lax.all_to_all(pieces, 'req', split_axis=0, concat_axis=0, tiled=True)]
    reduce_scatter x1 -> x0, waiting for transfers between devices: 31.6 us -> none  [shards(): lax.psum_scatter(jnp.einsum('tre,ed->trd', attended, output_weight, prefe...]
    ppermute x0 -> x6, waiting for transfers between devices: none -> 31.5 us  [swap(): return lax.ppermute(x, axis, [(i, i ^ bits) for i in range(size)])]
    reduce_sum x9 -> x1, other arithmetic: 21.5 us -> 0.63 us  [shards(): jnp.sum(jnp.where(slot_request[None, :] == slots[:, None], slots[None, :]...]
    scatter x6 -> x0, local copies, waits for them, and re-layouts: 10.4 us -> none  [the longest x5 9.84 us: shards(): initial.at[indices].set(fresh_rows)]
    lt x8 -> x0, other arithmetic: 5.92 us -> none  [visit(): allowed = (offset + jnp.arange(KEY_BLOCK))[None, :] < cache_lengths[:, None]]
  transfers between devices with their start and end apart: 5 -> 9, of which waited for: 5 -> 6; matrix products, arithmetic and copies ran while one was open for 7% -> 3% of each run, Pallas kernels for 0% -> 2%
where the time goes in v1:
time: 210 us
  waiting for transfers between devices  72.3 us (34%)
  starting transfers between devices  53.3 us (25%)
  Pallas kernels  47.3 us (23%)
  blocking collectives  21.7 us (10%)
  other arithmetic  8.92 us (4%)
  local copies, waits for them, and re-layouts  3.26 us (2%)
    all_to_all x3, starting transfers between devices, spread(): lax.all_to_all(pieces, 'req', split_axis=0, concat_axis=0, tiled=True)  49.6 us
    all_to_all x3, waiting for transfers between devices, spread(): lax.all_to_all(pieces, 'req', split_axis=0, concat_axis=0, tiled=True)  40.9 us
    pallas_call x1, Pallas kernels, attend(): pl.pallas_call(functools.partial(att_kernel, portion, chunk, chunks), out...  36.5 us
    ppermute x6, waiting for transfers between devices, swap(): return lax.ppermute(x, axis, [(i, i ^ bits) for i in range(size)])  31.5 us
    all_to_all x1, blocking collectives, spread(): lax.all_to_all(pieces, 'req', split_axis=0, concat_axis=0, tiled=True)  21.7 us
    pallas_call x1, Pallas kernels, prep(): pl.pallas_call(prep_kernel, out_shape=(out, out), in_specs=[SM] + [VM] *...  4.59 us
  transfers between devices with their start and end apart: 9, of which 6 were waited for; matrix products, arithmetic and copies ran while one was open for 3% of the time, Pallas kernels for 2%

profile of v1, /device:TPU:0, one launch (start us, length us, event | category | flops | bytes accessed | tf_op | source)
XLA Modules:
  0.0 209.7 jit_solution(113844271313112444)
XLA Ops:
  0.6 0.0 copy-start
  0.6 1.4 multiply_reduce_fusion
  2.0 0.1 rsqrt.12
  2.1 1.3 multiply_convert_fusion
  3.4 21.7 %all_to_all.20.x = bf16[8,16,2048]{2,1,0:T(8,128)(2,1)} all-to-all(bf16[8,16,2048]{2,1,0:T(8,128)(2,1)S(1)} %multiply_convert_fusion), channel_id=1, replica_groups=mesh['req'=8,'head'=4] {'req'}, dimensions={0} | all-to-all | bytes 1048576 | tf_op jit(solution)/shard_map/all_to_all | solution.py:294
  25.1 1.9 pick.2
  27.0 3.7 %all-to-all-start.1 = ((bf16[8,16,2048]{2,1,0:T(8,128)(2,1)}), bf16[8,16,2048]{2,1,0:T(8,128)(2,1)S(1)}, u32[]{:S(2)}, u32[]{:S(2)}) async-start(bf16[8,16,2048]{2,1,0:T(8,128)(2,1)} %pick.2), calls=%async_computation.1 | async-start | bytes 1048576 | tf_op jit(solution)/shard_map/all_to_all | solution.py:294
  31.4 0.0 copy-done.2
  31.4 0.1 add_bitcast_fusion
  31.5 13.4 %all-to-all-done.1 = bf16[8,16,2048]{2,1,0:T(8,128)(2,1)S(1)} async-done(((bf16[8,16,2048]{2,1,0:T(8,128)(2,1)}), bf16[8,16,2048]{2,1,0:T(8,128)(2,1)S(1)}, u32[]{:S(2)}, u32[]{:S(2)}) %all-to-all-start.1) | async-done | bytes 524320 | tf_op jit(solution)/shard_map/all_to_all | solution.py:294
  44.9 1.5 collective-permute-start.1
  46.4 0.1 pad_add_fusion.scal
  46.5 0.8 fusion.2
  47.2 1.0 fusion.1
  48.2 0.1 collective-permute-start
  48.3 8.7 %collective-permute-done.1.refs_2_ = bf16[128,2048]{1,0:T(8,128)(2,1)S(1)} collective-permute-done((bf16[128,2048]{1,0:T(8,128)(2,1)S(1)}, bf16[128,2048]{1,0:T(8,128)(2,1)S(1)}, u32[]{:S(2)}, u32[]{:S(2)}) %collective-permute-start.1) | collective-permute-done | bytes 524320 | tf_op jit(solution)/shard_map/ppermute | solution.py:287
  57.0 0.0 collective-permute-start.2
  57.0 0.4 pad_maximum_fusion.2
  57.4 0.5 pad_maximum_fusion
  58.0 0.0 copy-start.8
  58.0 1.0 copy-done.8
  59.0 4.6 %prep.1 = (bf16[2,4096,128]{2,1,0:T(8,128)(2,1)S(1)}, bf16[2,4096,128]{2,1,0:T(8,128)(2,1)S(1)}) custom-call(s32[1]{0:T(128)S(6)} %copy.17.length, bf16[384,2048]{1,0:T(8,128)(2,1)S(1)} %bitcast.36, f32[1,2048]{1,0:T(1,128)S(1)} %bitcast.35, bf16[2048,128]{1,0:T(8,128)(2,1)S(1)} %copy-done.7, bf16[2048,128]{1,0:T(8,128)(2,1)S(1)} %copy-done.8, ...), custom_call_target="tpu_custom_call" | custom-call | flops 3000000000 | bytes 8388608 | tf_op jit(solution)/shard_map/prep/pallas_call | solution.py:84
  63.6 0.0 collective-permute-done.refs_1_
  63.6 0.0 collective-permute-done.2.refs_3_
  63.6 2.4 %qkv.1 = (bf16[512,512]{1,0:T(8,128)(2,1)S(1)}, bf16[512,128]{1,0:T(8,128)(2,1)S(1)}, bf16[512,128]{1,0:T(8,128)(2,1)S(1)}) custom-call(bf16[128,2048]{1,0:T(8,128)(2,1)S(1)} %bitcast.32, bf16[128,2048]{1,0:T(8,128)(2,1)S(1)} %collective-permute-done.refs_1_, bf16[128,2048]{1,0:T(8,128)(2,1)S(1)} %collective-permute-done.1.refs_2_, ...), custom_call_target="tpu_custom_call" | custom-call | flops 1610612736 | bytes 5242880 | tf_op jit(solution)/shard_map/qkv/pallas_call | solution.py:115
  66.1 36.5 %attend.1 = bf16[512,512]{1,0:T(8,128)(2,1)S(1)} custom-call(s32[2]{0:T(128)S(1)} %pad_add_fusion.scal, bf16[512,512]{1,0:T(8,128)(2,1)S(1)} %get-tuple-element.9.q, bf16[2,4096,128]{2,1,0:T(8,128)(2,1)S(1)} %get-tuple-element.10.ka, bf16[2,4096,128]{2,1,0:T(8,128)(2,1)S(1)} %get-tuple-element.11.va, bf16[512,128]{1,0:T(8,128)(2,1)S(1)} %get-tuple-element.12.refs_0_, ...), custom_call_target="tpu_custom_call" | custom-call | flops 9663676416 | bytes 6291456 | tf_op jit(solution)/shard_map/attend/pallas_call | solution.py:239
  102.6 1.3 convolution_convert_fusion
  103.9 0.2 fusion.4
  104.1 0.0 copy-start.11
  104.1 0.6 collective-permute-start.3
  104.6 1.5 collective-permute-start.4
  106.2 0.0 collective-permute-start.5
  106.2 0.0 collective-permute-done.3
  106.2 13.2 %collective-permute-done.4 = bf16[128,2048]{1,0:T(8,128)(2,1)S(1)} collective-permute-done((bf16[128,2048]{1,0:T(8,128)(2,1)S(1)}, bf16[128,2048]{1,0:T(8,128)(2,1)S(1)}, u32[]{:S(2)}, u32[]{:S(2)}) %collective-permute-start.4) | collective-permute-done | bytes 524320 | tf_op jit(solution)/shard_map/ppermute | solution.py:287
  119.4 9.5 %collective-permute-done.5 = bf16[128,2048]{1,0:T(8,128)(2,1)S(1)} collective-permute-done((bf16[128,2048]{1,0:T(8,128)(2,1)S(1)}, bf16[128,2048]{1,0:T(8,128)(2,1)S(1)}, u32[]{:S(2)}, u32[]{:S(2)}) %collective-permute-start.5) | collective-permute-done | bytes 524320 | tf_op jit(solution)/shard_map/ppermute | solution.py:287
  128.9 1.1 add_convert_fusion
  130.0 42.2 %all-to-all-start.2 = ((bf16[8,16,2048]{2,1,0:T(8,128)(2,1)}), bf16[8,16,2048]{2,1,0:T(8,128)(2,1)S(1)}, u32[]{:S(2)}, u32[]{:S(2)}) async-start(bf16[8,16,2048]{2,1,0:T(8,128)(2,1)} %bitcast.9), calls=%async_computation.2 | async-start | bytes 1048576 | tf_op jit(solution)/shard_map/all_to_all | solution.py:294
  172.3 0.6 select_reduce_fusion.order
  172.9 14.8 %all-to-all-done.2.x = bf16[8,16,2048]{2,1,0:T(8,128)(2,1)S(1)} async-done(((bf16[8,16,2048]{2,1,0:T(8,128)(2,1)}), bf16[8,16,2048]{2,1,0:T(8,128)(2,1)S(1)}, u32[]{:S(2)}, u32[]{:S(2)}) %all-to-all-start.2) | async-done | bytes 524320 | tf_op jit(solution)/shard_map/all_to_all | solution.py:294
  187.7 0.8 copy-done.10
  188.5 1.9 pick.3
  190.3 3.7 %all-to-all-start.3 = ((bf16[8,16,2048]{2,1,0:T(8,128)(2,1)}), bf16[8,16,2048]{2,1,0:T(8,128)(2,1)S(1)}, u32[]{:S(2)}, u32[]{:S(2)}) async-start(bf16[8,16,2048]{2,1,0:T(8,128)(2,1)} %pick.3), calls=%async_computation.3 | async-start | bytes 1048576 | tf_op jit(solution)/shard_map/all_to_all | solution.py:294
  194.0 0.6 gather_fusion
  194.6 0.6 gather_fusion.1
  195.2 0.8 bitcast_select_fusion
  196.0 12.7 %all-to-all-done.3 = bf16[8,16,2048]{2,1,0:T(8,128)(2,1)S(1)} async-done(((bf16[8,16,2048]{2,1,0:T(8,128)(2,1)}), bf16[8,16,2048]{2,1,0:T(8,128)(2,1)S(1)}, u32[]{:S(2)}, u32[]{:S(2)}) %all-to-all-start.3) | async-done | bytes 524320 | tf_op jit(solution)/shard_map/all_to_all | solution.py:294
  208.7 0.0 copy-done.9
  208.7 0.9 fusion
  (24 shorter events, 0.1 us)
Async XLA Ops:
  0.6 101.9 %copy-start = (bf16[512,2048]{1,0:T(8,128)(2,1)S(1)}, bf16[512,2048]{1,0:T(8,128)(2,1)}, u32[]{:S(2)}) copy-start(bf16[512,2048]{1,0:T(8,128)(2,1)} %param.19) | copy-start | bytes 6291460
  2.1 29.3 %copy-start.2 = (s32[1,384]{1,0:T(1,128)S(1)}, s32[1,384]{1,0:T(1,128)}, u32[]{:S(2)}) copy-start(s32[1,384]{1,0:T(1,128)} %index.1) | copy-start | bytes 4612
  27.0 30.9 %copy-start.7 = (bf16[2048,128]{1,0:T(8,128)(2,1)S(1)}, bf16[2048,128]{1,0:T(8,128)(2,1)}, u32[]{:S(2)}) copy-start(bf16[2048,128]{1,0:T(8,128)(2,1)} %wk.1) | copy-start | bytes 1572868
  27.0 17.9 %all-to-all-start.1 = ((bf16[8,16,2048]{2,1,0:T(8,128)(2,1)}), bf16[8,16,2048]{2,1,0:T(8,128)(2,1)S(1)}, u32[]{:S(2)}, u32[]{:S(2)}) async-start(bf16[8,16,2048]{2,1,0:T(8,128)(2,1)} %pick.2), calls=%async_computation.1 | async-start | bytes 1048576 | tf_op jit(solution)/shard_map/all_to_all | solution.py:294
  30.7 27.2 %copy-start.1 = (f32[2048]{0:T(1024)S(1)}, f32[2048]{0:T(1024)}, u32[]{:S(2)}) copy-start(f32[2048]{0:T(1024)} %param.15) | copy-start | bytes 24580
  44.9 13.1 %copy-start.4 = (bf16[1,384,2048]{2,1,0:T(8,128)(2,1)S(1)}, bf16[1,384,2048]{2,1,0:T(8,128)(2,1)}, u32[]{:S(2)}) copy-start(bf16[1,384,2048]{2,1,0:T(8,128)(2,1)} %param.22) | copy-start | bytes 4718596
  44.9 13.1 %copy-start.5 = (bf16[1,4096,128]{2,1,0:T(8,128)(2,1)S(1)}, bf16[1,4096,128]{2,1,0:T(8,128)(2,1)}, u32[]{:S(2)}) copy-start(bf16[1,4096,128]{2,1,0:T(8,128)(2,1)} %param.20) | copy-start | bytes 3145732
  44.9 13.1 %copy-start.6 = (bf16[1,4096,128]{2,1,0:T(8,128)(2,1)S(1)}, bf16[1,4096,128]{2,1,0:T(8,128)(2,1)}, u32[]{:S(2)}) copy-start(bf16[1,4096,128]{2,1,0:T(8,128)(2,1)} %param.21) | copy-start | bytes 3145732
  44.9 12.2 %collective-permute-start.1 = (bf16[128,2048]{1,0:T(8,128)(2,1)S(1)}, bf16[128,2048]{1,0:T(8,128)(2,1)S(1)}, u32[]{:S(2)}, u32[]{:S(2)}) collective-permute-start(bf16[128,2048]{1,0:T(8,128)(2,1)S(1)} %bitcast.30), channel_id=1, source_target_pairs={{0,2},{1,3},{2,0},{3,1},{4,6},{5,7},{6,4},{7,5},{8,10},{9,11},{10,... | collective-permute-start | bytes 1572872 | tf_op jit(solution)/shard_map/ppermute | solution.py:287
  48.2 15.4 %collective-permute-start = (bf16[128,2048]{1,0:T(8,128)(2,1)S(1)}, bf16[128,2048]{1,0:T(8,128)(2,1)S(1)}, u32[]{:S(2)}, u32[]{:S(2)}) collective-permute-start(bf16[128,2048]{1,0:T(8,128)(2,1)S(1)} %bitcast.31), channel_id=1, source_target_pairs={{0,1},{1,0},{2,3},{3,2},{4,5},{5,4},{6,7},{7,6},{8,9},{9,8},{10,11... | collective-permute-start | bytes 1572872 | tf_op jit(solution)/shard_map/ppermute | solution.py:287
  57.0 6.6 %collective-permute-start.2 = (bf16[128,2048]{1,0:T(8,128)(2,1)S(1)}, bf16[128,2048]{1,0:T(8,128)(2,1)S(1)}, u32[]{:S(2)}, u32[]{:S(2)}) collective-permute-start(bf16[128,2048]{1,0:T(8,128)(2,1)S(1)} %collective-permute-done.1.refs_2_), channel_id=1, source_target_pairs={{0,1},{1,0},{2,3},{3,2},{4,5},{5,4},{6,7},{7,6},{8,9},{9,8},{10,11... | collective-permute-start | bytes 1572872 | tf_op jit(solution)/shard_map/ppermute | solution.py:287
  58.0 1.0 copy-start.8
  59.0 4.6 %copy-start.3 = (bf16[2048,512]{1,0:T(8,128)(2,1)S(1)}, bf16[2048,512]{1,0:T(8,128)(2,1)}, u32[]{:S(2)}) copy-start(bf16[2048,512]{1,0:T(8,128)(2,1)} %refs_4_.1) | copy-start | bytes 6291460
  104.1 68.2 %copy-start.11 = (s32[8]{0:T(128)S(1)}, s32[8]{0:T(128)}, u32[]{:S(2)}) copy-start(s32[8]{0:T(128)} %order.1) | copy-start | bytes 100
  104.1 2.1 %collective-permute-start.3 = (bf16[128,2048]{1,0:T(8,128)(2,1)S(1)}, bf16[128,2048]{1,0:T(8,128)(2,1)S(1)}, u32[]{:S(2)}, u32[]{:S(2)}) collective-permute-start(bf16[128,2048]{1,0:T(8,128)(2,1)S(1)} %get-tuple-element.14), channel_id=1, source_target_pairs={{0,1},{1,0},{2,3},{3,2},{4,5},{5,4},{6,7},{7,6},{8,9},{9,8},{10,11... | collective-permute-start | bytes 1572872 | tf_op jit(solution)/shard_map/ppermute | solution.py:287
  104.6 14.8 %collective-permute-start.4 = (bf16[128,2048]{1,0:T(8,128)(2,1)S(1)}, bf16[128,2048]{1,0:T(8,128)(2,1)S(1)}, u32[]{:S(2)}, u32[]{:S(2)}) collective-permute-start(bf16[128,2048]{1,0:T(8,128)(2,1)S(1)} %get-tuple-element.16), channel_id=1, source_target_pairs={{0,2},{1,3},{2,0},{3,1},{4,6},{5,7},{6,4},{7,5},{8,10},{9,11},{10,... | collective-permute-start | bytes 1572872 | tf_op jit(solution)/shard_map/ppermute | solution.py:287
  106.2 22.7 %collective-permute-start.5 = (bf16[128,2048]{1,0:T(8,128)(2,1)S(1)}, bf16[128,2048]{1,0:T(8,128)(2,1)S(1)}, u32[]{:S(2)}, u32[]{:S(2)}) collective-permute-start(bf16[128,2048]{1,0:T(8,128)(2,1)S(1)} %get-tuple-element.15), channel_id=1, source_target_pairs={{0,3},{1,2},{2,1},{3,0},{4,7},{5,6},{6,5},{7,4},{8,11},{9,10},{10,... | collective-permute-start | bytes 1572872 | tf_op jit(solution)/shard_map/ppermute | solution.py:287
  130.0 78.7 %copy-start.9 = (bf16[1,128,2048]{2,1,0:T(8,128)(2,1)S(1)}, bf16[1,128,2048]{2,1,0:T(8,128)(2,1)}, u32[]{:S(2)}) copy-start(bf16[1,128,2048]{2,1,0:T(8,128)(2,1)} %param.14) | copy-start | bytes 1572868
  130.0 57.6 %all-to-all-start.2 = ((bf16[8,16,2048]{2,1,0:T(8,128)(2,1)}), bf16[8,16,2048]{2,1,0:T(8,128)(2,1)S(1)}, u32[]{:S(2)}, u32[]{:S(2)}) async-start(bf16[8,16,2048]{2,1,0:T(8,128)(2,1)} %bitcast.9), calls=%async_computation.2 | async-start | bytes 1048576 | tf_op jit(solution)/shard_map/all_to_all | solution.py:294
  187.7 0.8 copy-start.10
  190.3 18.4 %all-to-all-start.3 = ((bf16[8,16,2048]{2,1,0:T(8,128)(2,1)}), bf16[8,16,2048]{2,1,0:T(8,128)(2,1)S(1)}, u32[]{:S(2)}, u32[]{:S(2)}) async-start(bf16[8,16,2048]{2,1,0:T(8,128)(2,1)} %pick.3), calls=%async_computation.3 | async-start | bytes 1048576 | tf_op jit(solution)/shard_map/all_to_all | solution.py:294

commit v2 on v1

v2 whole, which is shorter than its diff:
```python
import functools, math
import jax
import jax.numpy as jnp
from jax import lax
from jax.experimental import pallas as pl
from jax.experimental.pallas import tpu as pltpu
from jax.sharding import PartitionSpec as P

HD = 64
LANES = 128
F32 = jnp.float32
BF16 = jnp.bfloat16
ROPE_BASE = 500000.0
MASKED = -1e30
TOP = 2.0**100
FACTOR = HD**-0.5 * math.log2(math.e)
NT = (((1,), (1,)), ((), ()))
VM = pl.BlockSpec(memory_space=pltpu.VMEM)
SM = pl.BlockSpec(memory_space=pltpu.SMEM)


def hbm(x):
    return pltpu.with_memory_space_constraint(x, pltpu.HBM)


def rms_scaled(values, gains):
    factor = lax.rsqrt(jnp.mean(values * values, axis=-1, keepdims=True) + 1e-05)
    return (values * factor * gains).astype(BF16)


def lane_of(shape):
    return lax.broadcasted_iota(jnp.int32, shape, len(shape) - 1)


def turned(x, cosine, sine):
    lane = lane_of(x.shape)
    swapped = jnp.where(
        lane % HD < HD // 2, pltpu.roll(x, LANES - HD // 2, 1), pltpu.roll(x, HD // 2, 1)
    )
    return x * cosine + swapped * sine


def head_lanes(x, which):
    return x if which == 0 else pltpu.roll(x, HD, 1)


def key_rows(k, which, bias):
    lane = lane_of(k.shape)
    tail = jnp.where(lane == HD, 1.0, jnp.where(lane == HD + 1, bias, 0.0))
    return jnp.where(lane < HD, head_lanes(k, which), tail).astype(BF16)


def value_rows(v, which):
    lane = lane_of(v.shape)
    return jnp.where(lane < HD, head_lanes(v, which), jnp.where(lane == HD, 1.0, 0.0)).astype(BF16)


def prep_kernel(length, held, gain, wk, wv, cosine, sine, index, ck, cv, ka, va, fresh):
    normed = rms_scaled(held[...].astype(F32), gain[...])
    k = jnp.dot(normed, wk[...], preferred_element_type=F32)
    fresh[:, :LANES] = turned(k, cosine[...], sine[...]).astype(BF16)
    fresh[:, LANES:] = jnp.dot(normed, wv[...], preferred_element_type=F32).astype(BF16)
    step = 512
    count = held.shape[0]

    def body(b, _):
        base = pl.multiple_of(b * step, step)
        rows = lax.broadcasted_iota(jnp.int32, (step, count), 0) + base
        hit = (rows == index[...]).astype(F32)
        placed = jnp.dot(hit.astype(BF16), fresh[...], preferred_element_type=F32)
        taken = jnp.max(hit, axis=1, keepdims=True) > 0.0
        at = pl.ds(base, step)
        kk = jnp.where(taken, placed[:, :LANES], ck[at, :].astype(F32))
        vv = jnp.where(taken, placed[:, LANES:], cv[at, :].astype(F32))
        row = lax.broadcasted_iota(jnp.int32, (step, LANES), 0) + base
        bias = jnp.where(row < length[0], 0.0, MASKED)
        for j in range(2):
            ka[j, at, :] = key_rows(kk, j, bias)
            va[j, at, :] = value_rows(vv, j)
        return 0

    lax.fori_loop(0, ck.shape[0] // step, body, 0)


def prep(length, held, gain, wk, wv, cosine, sine, index, ck, cv):
    cap = ck.shape[0]
    out = jax.ShapeDtypeStruct((2, cap, LANES), BF16)
    return pl.pallas_call(
        prep_kernel,
        out_shape=(out, out),
        in_specs=[SM] + [VM] * 9,
        out_specs=(VM, VM),
        scratch_shapes=[pltpu.VMEM((held.shape[0], 2 * LANES), BF16)],
        compiler_params=pltpu.CompilerParams(vmem_limit_bytes=40 << 20),
        cost_estimate=pl.CostEstimate(flops=3 * 10**9, bytes_accessed=8 << 20, transcendentals=0),
        name="prep",
    )(length, held, gain, wk, wv, cosine, sine, index, ck, cv)


def qkv_kernel(pieces, *refs):
    xs, (wq, wk, wv, cosine, sine, q, k, v, x, bq, bk, bv, done) = refs[:pieces], refs[pieces:]
    rows = xs[0].shape[0]
    copies = [
        pltpu.make_async_copy(piece, x.at[i * rows : (i + 1) * rows, :], done.at[i])
        for i, piece in enumerate(xs)
    ]
    for i, (w, buffer) in enumerate(((wk, bk), (wv, bv), (wq, bq))):
        copies.append(pltpu.make_async_copy(w, buffer, done.at[pieces + i]))
    for copy in copies:
        copy.start()
    c, s = cosine[...], sine[...]
    for copy in copies[: pieces + 1]:
        copy.wait()
    xv = x[...]
    k[...] = turned(jnp.dot(xv, bk[...], preferred_element_type=F32), c, s).astype(BF16)
    copies[pieces + 1].wait()
    v[...] = jnp.dot(xv, bv[...], preferred_element_type=F32).astype(BF16)
    copies[pieces + 2].wait()
    for j in range(wq.shape[1] // 256):
        got = jnp.dot(xv, bq[:, j * 256 : (j + 1) * 256], preferred_element_type=F32)
        for t in range(2):
            at = slice(j * 256 + t * LANES, j * 256 + (t + 1) * LANES)
            q[:, at] = turned(got[:, t * LANES : (t + 1) * LANES], c, s).astype(BF16)


def qkv(xs, wq, wk, wv, cosine, sine):
    rows = sum(x.shape[0] for x in xs)
    depth, width = wq.shape
    out = lambda n: jax.ShapeDtypeStruct((rows, n), BF16)
    raw = pl.BlockSpec(memory_space=pltpu.HBM)
    any_place = pl.BlockSpec(memory_space=pl.ANY)
    return pl.pallas_call(
        functools.partial(qkv_kernel, len(xs)),
        out_shape=(out(width), out(LANES), out(LANES)),
        in_specs=[any_place] * len(xs) + [raw] * 3 + [VM] * 2,
        out_specs=(VM,) * 3,
        scratch_shapes=[
            pltpu.VMEM((rows, depth), BF16),
            pltpu.VMEM((depth, width), BF16),
            pltpu.VMEM((depth, LANES), BF16),
            pltpu.VMEM((depth, LANES), BF16),
            pltpu.SemaphoreType.DMA((len(xs) + 3,)),
        ],
        compiler_params=pltpu.CompilerParams(vmem_limit_bytes=16 << 20),
        cost_estimate=pl.CostEstimate(
            flops=2 * rows * depth * (width + 2 * LANES), bytes_accessed=5 << 20, transcendentals=0
        ),
        name="qkv",
    )(*xs, hbm(wq), hbm(wk), hbm(wv), cosine, sine)


KEYS = 1024
ROWS = 1024
CHUNKS = 1


def att_kernel(portion, chunk, chunks, js, mode, scal, q, ka, va, *refs):
    refs = list(refs)
    take_refs = lambda count: [refs.pop(0) for _ in range(count)]
    if mode != "cached":
        kn, vn = take_refs(chunks), take_refs(chunks)
    if mode == "new":
        qa_in, acc_in = take_refs(2)
    if mode == "cached":
        qa_out, acc_out = take_refs(2)
    else:
        (o,) = take_refs(1)
    if mode != "cached":
        qa_s, acc_s, na, nv, low = take_refs(5)
    if mode == "new":
        kbuf, vbuf = take_refs(2)
    tokens = q.shape[0]
    length, head = scal[0], scal[1]
    per = q.shape[1] // HD // 2
    rows = per * tokens
    blocks = lax.div(length + (KEYS - 1), KEYS)
    lane = lane_of((tokens, LANES))
    spans = [slice(g * tokens, (g + 1) * tokens) for g in range(per)]

    def token(i, part):
        which = lax.div(i, portion)
        swapped = which if mode is None else lax.div(which, 2) + 2 * lax.rem(which, 2)
        return (swapped ^ head) * (portion * chunks) + part * portion + (i - which * portion)

    if mode != "cached":
        own = token(lax.broadcasted_iota(jnp.int32, (tokens, tokens), 0), chunk)
        allowed = [
            token(lax.broadcasted_iota(jnp.int32, (tokens, tokens), 1), part) <= own
            for part in range(chunks)
        ]

    for n, j in enumerate(js):
        if mode == "cached":
            qa, acc = qa_out.at[n], acc_out.at[n]
        else:
            qa, acc = qa_s, acc_s

        def put_queries(g, offset):
            pair = (j * per + g) // 2
            x = q[:, pair * LANES : (pair + 1) * LANES].astype(F32)
            tail = jnp.where(lane == HD, offset, jnp.where(lane == HD + 1, 1.0, 0.0))
            qa[spans[g], :] = jnp.where(lane < HD, head_lanes(x, g % 2), tail).astype(BF16)

        def weights(keys, at):
            s = lax.dot_general(qa[at, :], keys, NT, preferred_element_type=F32)
            return jnp.exp2(s * FACTOR)

        if mode == "new":
            qa[...] = qa_in[n]
            acc[...] = acc_in[n]
        else:
            for g in range(per):
                put_queries(g, 0.0)
                first = lax.dot_general(
                    qa[spans[g], :], ka[j, :256, :], NT, preferred_element_type=F32
                )
                put_queries(g, -jnp.max(first, axis=1, keepdims=True))
            acc[...] = jnp.zeros(acc.shape, F32)

        if mode != "cached":
            for part in range(chunks):
                na[part] = key_rows(kn[part][...].astype(F32), j, 0.0)
                nv[part] = value_rows(vn[part][...].astype(F32), j)
            for g in range(per):
                total = acc[spans[g], :]
                for part in range(chunks):
                    p = jnp.where(allowed[part], weights(na[part], spans[g]), 0.0)
                    total += jnp.dot(p.astype(BF16), nv[part], preferred_element_type=F32)
                acc[spans[g], :] = total

        if mode != "new":

            def body(b, _):
                at = pl.ds(pl.multiple_of(b * KEYS, KEYS), KEYS)
                keys, values = ka[j, at, :], va[j, at, :]
                for r in range(rows // ROWS):
                    q_at = slice(r * ROWS, (r + 1) * ROWS)
                    p = weights(keys, q_at).astype(BF16)
                    acc[q_at, :] += jnp.dot(p, values, preferred_element_type=F32)
                return 0

            lax.fori_loop(0, blocks, body, 0)

        if mode == "cached":
            continue

        safe = jnp.min((acc[:, HD : HD + 1] < TOP).astype(F32)) > 0.5

        @pl.when(jnp.logical_not(safe))
        def _():
            if mode == "new":
                pltpu.sync_copy(ka.at[j], kbuf)
                pltpu.sync_copy(va.at[j], vbuf)
                old_k, old_v = kbuf, vbuf
            else:
                old_k, old_v = ka.at[j], va.at[j]
            for g in range(per):
                put_queries(g, 0.0)
            acc[...] = jnp.zeros(acc.shape, F32)
            low[...] = jnp.full(low.shape, MASKED, F32)

            def take(keys, values, permitted, at):
                s = lax.dot_general(qa[at, :], keys, NT, preferred_element_type=F32)
                if permitted is not None:
                    s = jnp.where(permitted, s, MASKED)
                past = low[at, :]
                top = jnp.maximum(past, jnp.max(s, axis=1, keepdims=True))
                p = jnp.exp2((s - top[:, :1]) * FACTOR)
                shrink = jnp.exp2((past - top) * FACTOR)
                low[at, :] = top
                acc[at, :] = acc[at, :] * shrink + jnp.dot(
                    p.astype(BF16), values, preferred_element_type=F32
                )

            def redo(b, _):
                at = pl.ds(pl.multiple_of(b * 512, 512), 512)
                for g in range(per):
                    take(old_k[at, :], old_v[at, :], None, spans[g])
                return 0

            lax.fori_loop(0, lax.div(length + 511, 512), redo, 0)
            for g in range(per):
                for part in range(chunks):
                    take(na[part], nv[part], allowed[part], spans[g])

        for g in range(0, per, 2):
            pair = []
            for t in range(2):
                got = acc[spans[g + t], :]
                pair.append(got / got[:, HD : HD + 1])
            at = slice((n * per + g) * HD, (n * per + g + 2) * HD)
            o[:, at] = jnp.where(lane < HD, pair[0], pltpu.roll(pair[1], HD, 1)).astype(BF16)


def attend(portion, chunk, js, mode, scal, q, ka, va, kns=(), vns=(), began=()):
    tokens, chunks = q.shape[0], CHUNKS
    rows = q.shape[1] // HD // 2 * tokens
    keys = {"cached": ka.shape[1], "new": tokens * chunks, "full": ka.shape[1] + tokens * chunks}[mode]
    scratch = []
    if mode != "cached":
        scratch = [
            pltpu.VMEM((rows, LANES), BF16),
            pltpu.VMEM((rows, LANES), F32),
            pltpu.VMEM((chunks, tokens, LANES), BF16),
            pltpu.VMEM((chunks, tokens, LANES), BF16),
            pltpu.VMEM((rows, LANES), F32),
        ]
    cached = VM
    if mode == "new":
        scratch += [pltpu.VMEM(ka.shape[1:], BF16)] * 2
        cached = pl.BlockSpec(memory_space=pl.ANY)
    if mode == "cached":
        shape = (len(js), rows, LANES)
        out = (jax.ShapeDtypeStruct(shape, BF16), jax.ShapeDtypeStruct(shape, F32))
        specs = (VM, VM)
    else:
        out = jax.ShapeDtypeStruct((tokens, q.shape[1] // 2 * len(js)), BF16)
        specs = VM
    return pl.pallas_call(
        functools.partial(att_kernel, portion, chunk, chunks, js, mode),
        out_shape=out,
        in_specs=[SM, VM, cached, cached] + [VM] * (len(kns) + len(vns) + len(began)),
        out_specs=specs,
        scratch_shapes=scratch,
        compiler_params=pltpu.CompilerParams(vmem_limit_bytes=32 << 20),
        cost_estimate=pl.CostEstimate(
            flops=4 * rows * len(js) * keys * 256,
            bytes_accessed=4 << 20,
            transcendentals=rows * len(js) * keys,
        ),
        name="attend_" + mode,
    )(scal, q, ka, va, *kns, *vns, *began)


def tables(positions):
    ladder = jnp.arange(HD // 2).astype(F32)
    frequency = jnp.exp(ladder * (-2.0 * math.log(ROPE_BASE) / HD))
    angles = positions[:, None] * frequency
    cosine, sine = jnp.cos(angles), jnp.sin(angles)
    return (
        jnp.concatenate([cosine] * 4, axis=-1),
        jnp.concatenate([-sine, sine, -sine, sine], axis=-1),
    )


def pick_kernel(order, x, out, done):
    count = out.shape[0]
    copies = [pltpu.make_async_copy(x.at[order[s]], out.at[s], done.at[s]) for s in range(count)]
    for copy in copies:
        copy.start()
    for copy in copies:
        copy.wait()


def pick(x, order):
    return pl.pallas_call(
        pick_kernel,
        out_shape=jax.ShapeDtypeStruct(x.shape, x.dtype),
        in_specs=[SM, pl.BlockSpec(memory_space=pl.ANY)],
        out_specs=pl.BlockSpec(memory_space=pl.ANY),
        scratch_shapes=[pltpu.SemaphoreType.DMA((x.shape[0],))],
        compiler_params=pltpu.CompilerParams(vmem_limit_bytes=1 << 20),
        name="pick",
    )(order, x)


def pick_norm_kernel(order, x, gain, out):
    for s in range(out.shape[0]):
        out[s] = rms_scaled(x[order[s]].astype(F32), gain[...])


def pick_norm(x, order, gain):
    return pl.pallas_call(
        pick_norm_kernel,
        out_shape=jax.ShapeDtypeStruct(x.shape, x.dtype),
        in_specs=[SM, VM, VM],
        out_specs=VM,
        compiler_params=pltpu.CompilerParams(vmem_limit_bytes=8 << 20),
        name="pick_norm",
    )(order, x, gain)


def project_kernel(mine, theirs, w, w_pair, keep, send):
    terms = [
        jnp.dot(x[...], y[...], preferred_element_type=F32).astype(BF16).astype(F32)
        for x, y in ((mine, w), (theirs, w_pair))
    ]
    total = terms[0] + terms[1]
    half = keep.shape[0]
    keep[...] = total[:half]
    send[...] = total[half:].astype(BF16)


def project(mine, theirs, w, w_pair):
    rows, depth = mine.shape
    width = w.shape[1]
    step = 512
    half = rows // 2
    return pl.pallas_call(
        project_kernel,
        out_shape=(
            jax.ShapeDtypeStruct((half, width), F32),
            jax.ShapeDtypeStruct((half, width), BF16),
        ),
        grid=(width // step,),
        in_specs=[pl.BlockSpec((rows, depth), lambda n: (0, 0))] * 2
        + [pl.BlockSpec((depth, step), lambda n: (0, n))] * 2,
        out_specs=(pl.BlockSpec((half, step), lambda n: (0, n)),) * 2,
        compiler_params=pltpu.CompilerParams(vmem_limit_bytes=16 << 20),
        cost_estimate=pl.CostEstimate(
            flops=4 * rows * depth * width, bytes_accessed=6 << 20, transcendentals=0
        ),
        name="project",
    )(mine, theirs, w, w_pair)


def swap(x, axis, bits):
    size = lax.axis_size(axis)
    return lax.ppermute(x, axis, [(i, i ^ bits) for i in range(size)])


def spread(x):
    groups = lax.axis_size("req")
    rows, features = x.shape
    pieces = x.reshape(groups, rows // groups, features)
    return lax.all_to_all(pieces, "req", split_axis=0, concat_axis=0, tiled=True)


def shards(
    hidden_in,
    norm_gain,
    query_weight,
    key_weight,
    value_weight,
    output_weight,
    cache_keys,
    cache_values,
    held_states,
    cache_lengths,
    recompute_index,
    slot_request,
):
    requests_here, positions_here, features = hidden_in.shape
    assert requests_here == 1
    heads = lax.axis_size("head")
    head = lax.axis_index("head")
    portion = positions_here // CHUNKS
    mine = hidden_in[0]
    gain = norm_gain[None, :]
    length = cache_lengths[0]
    relative = jnp.arange(heads).reshape(2, heads // 2).T.reshape(-1) ^ head
    tables_of = [
        tables(
            (
                relative[:, None] * positions_here + part * portion + jnp.arange(portion)[None, :]
            ).reshape(-1).astype(F32)
            + length.astype(F32)
        )
        for part in range(CHUNKS)
    ]
    scal = jnp.stack([length, head.astype(jnp.int32)])
    tie = lax.optimization_barrier
    flat = lambda x: x.reshape(portion, features)
    far_bit, near_bit = heads // 2, 1
    w_pair = swap(output_weight, "head", near_bit)
    held_cos, held_sin = tables(recompute_index[0].astype(F32))

    def project_in(c, own):
        far = swap(own, "head", far_bit)
        near = swap(own, "head", near_bit)
        corner = swap(far, "head", near_bit)
        return qkv([own, far, near, corner], query_weight, key_weight, value_weight, *tables_of[c])

    def project_out(pieces):
        attended = pieces[0] if len(pieces) == 1 else jnp.concatenate(pieces, axis=1)
        theirs = swap(attended[2 * portion :], "head", near_bit)
        keep, send = project(attended[: 2 * portion], theirs, output_weight, w_pair)
        return keep, swap(send, "head", far_bit)

    join = lambda keep, got: (keep + got.astype(F32)).astype(BF16)
    slots = jnp.arange(slot_request.shape[0], dtype=jnp.int32)
    inverse = jnp.sum(jnp.where(slot_request[None, :] == slots[:, None], slots[None, :], 0), axis=1)

    ka, va = prep(
        cache_lengths,
        held_states[0],
        gain,
        key_weight,
        value_weight,
        held_cos,
        held_sin,
        recompute_index,
        cache_keys[0],
        cache_values[0],
    )
    first = spread(mine)
    first, ka, va, tables_of = tie((first, ka, va, tables_of))
    own = flat(spread(flat(pick_norm(first, slot_request, gain))))
    q, kn, vn = project_in(0, own)
    kns, vns = [kn], [vn]
    attended = attend(portion, 0, (0, 1), "full", scal, q, ka, va, kns, vns)
    back = spread(join(*project_out([attended])))
    returned = [flat(spread(flat(pick(back, inverse))))]
    returned = jnp.concatenate(returned, axis=0)
    hidden_out = (mine.astype(F32) + returned.astype(F32)).astype(BF16)

    away = jnp.arange(heads) ^ head

    def by_token(pieces):
        stacked = jnp.stack([x.reshape(heads, portion, LANES) for x in pieces], axis=1)
        return jnp.take(stacked, lax.div(away, 2) + 2 * lax.rem(away, 2), axis=0).reshape(1, heads * positions_here, LANES)

    return (hidden_out[None], by_token(kns), by_token(vns))


def solution(mesh):
    return jax.shard_map(
        shards,
        mesh=mesh,
        in_specs=(
            P("req", "head", None),
            P(),
            P(None, "head"),
            P(None, "head"),
            P(None, "head"),
            P("head", None),
            P("req", None, "head"),
            P("req", None, "head"),
            P("req", None, None),
            P("req"),
            P("req", None),
            P(),
        ),
        out_specs=(P("req", "head", None), P("req", None, "head"), P("req", None, "head")),
        check_vma=False,
    )
```

time: 210 us -> 193 us (0.919)
  waiting for transfers between devices: 72.3 us -> 52.1 us
  starting transfers between devices: 53.3 us -> 67.9 us
  Pallas kernels: 47.3 us -> 36.3 us
  local copies, waits for them, and re-layouts: 3.26 us -> 8.46 us
  other arithmetic: 8.92 us -> 6.35 us
    all_to_all x3, waiting for transfers between devices: 40.9 us -> 26.1 us  [spread(): lax.all_to_all(pieces, 'req', split_axis=0, concat_axis=0, tiled=True)]
    all_to_all x3, starting transfers between devices: 49.6 us -> 64.1 us  [spread(): lax.all_to_all(pieces, 'req', split_axis=0, concat_axis=0, tiled=True)]
    pallas_call x2 -> x4, Pallas kernels: 38.9 us -> 30.4 us  [the longest x1 21.9 us: attend(): pl.pallas_call(functools.partial(att_kernel, portion, chunk, chunks, js,...]
    ppermute x6, waiting for transfers between devices: 31.5 us -> 25.9 us  [swap(): return lax.ppermute(x, axis, [(i, i ^ bits) for i in range(size)])]
    unnamed x24 -> x28, local copies, waits for them, and re-layouts: 1.87 us -> 7.19 us
    pallas_call x2 -> x1, Pallas kernels: 3.77 us -> 1.39 us  [pick(): pl.pallas_call(pick_kernel, out_shape=jax.ShapeDtypeStruct(x.shape, x.dty...]
  transfers between devices with their start and end apart: 9 -> 9, of which waited for: 6 -> 6; matrix products, arithmetic and copies ran while one was open for 3% -> 3% of each run, Pallas kernels for 2% -> 17%
where the time goes in v2:
time: 193 us; the launch traced here: 192 us
  starting transfers between devices  67.9 us (35%)
  waiting for transfers between devices  52.1 us (27%)
  Pallas kernels  36.3 us (19%)
  blocking collectives  19.7 us (10%)
  local copies, waits for them, and re-layouts  8.46 us (4%)
  other arithmetic  6.35 us (3%)
    all_to_all x3, starting transfers between devices, spread(): lax.all_to_all(pieces, 'req', split_axis=0, concat_axis=0, tiled=True)  64.1 us
    all_to_all x3, waiting for transfers between devices, spread(): lax.all_to_all(pieces, 'req', split_axis=0, concat_axis=0, tiled=True)  26.1 us
    ppermute x6, waiting for transfers between devices, swap(): return lax.ppermute(x, axis, [(i, i ^ bits) for i in range(size)])  25.9 us
    pallas_call x1, Pallas kernels, attend(): pl.pallas_call(functools.partial(att_kernel, portion, chunk, chunks, js,...  21.9 us
    all_to_all x1, blocking collectives, spread(): lax.all_to_all(pieces, 'req', split_axis=0, concat_axis=0, tiled=True)  19.7 us
    unnamed x28, local copies, waits for them, and re-layouts  7.19 us
    pallas_call x1, Pallas kernels, qkv(): pl.pallas_call(functools.partial(qkv_kernel, len(xs)), out_shape=(out(wid...  5.49 us
    pallas_call x1, Pallas kernels, prep(): pl.pallas_call(prep_kernel, out_shape=(out, out), in_specs=[SM] + [VM] *...  4.57 us
  transfers between devices with their start and end apart: 9, of which 6 were waited for; matrix products, arithmetic and copies ran while one was open for 3% of the time, Pallas kernels for 17%

profile of v2, /device:TPU:0, one launch (start us, length us, event | category | flops | bytes accessed | tf_op | source)
XLA Modules:
  0.0 192.4 jit_solution(1016008386580690853)
XLA Ops:
  0.6 7.3 %all-to-all-start = ((bf16[8,16,2048]{2,1,0:T(8,128)(2,1)}), bf16[8,16,2048]{2,1,0:T(8,128)(2,1)S(1)}, u32[]{:S(2)}, u32[]{:S(2)}) async-start(bf16[8,16,2048]{2,1,0:T(8,128)(2,1)} %bitcast.37), calls=%async_computation | async-start | bytes 1048576 | tf_op jit(solution)/shard_map/all_to_all | solution.py:426
  7.9 0.0 copy-start.2
  7.9 0.0 copy-start.4
  7.9 0.8 convert_reduce_fusion
  8.8 0.8 fusion.2
  9.5 0.4 pad_maximum_fusion.2
  9.9 0.1 mul.56
  10.7 0.1 add_bitcast_fusion
  10.7 1.0 fusion.1
  11.7 0.5 pad_maximum_fusion
  12.2 0.0 copy-start.5
  12.2 1.2 copy-done.5
  13.5 1.2 copy-done.6
  14.7 1.0 copy-done.7
  15.7 1.0 copy-done.8
  16.8 4.6 %prep.1 = (bf16[2,4096,128]{2,1,0:T(8,128)(2,1)S(1)}, bf16[2,4096,128]{2,1,0:T(8,128)(2,1)S(1)}) custom-call(s32[1]{0:T(128)S(6)} %copy.17.length, bf16[384,2048]{1,0:T(8,128)(2,1)S(1)} %bitcast.34, f32[1,2048]{1,0:T(1,128)S(1)} %bitcast.32, bf16[2048,128]{1,0:T(8,128)(2,1)S(1)} %copy-done.7, bf16[2048,128]{1,0:T(8,128)(2,1)S(1)} %copy-done.8, ...), custom_call_target="tpu_custom_call" | custom-call | flops 3000000000 | bytes 8388608 | tf_op jit(solution)/shard_map/prep/pallas_call | solution.py:88
  21.4 1.3 copy-done.9
  22.7 1.3 copy-done.11
  24.0 0.0 all-to-all-done.x
  24.0 0.8 pick_norm.1
  24.8 19.7 %all_to_all.20 = bf16[8,16,2048]{2,1,0:T(8,128)(2,1)S(1)} all-to-all(bf16[8,16,2048]{2,1,0:T(8,128)(2,1)S(1)} %pick_norm.1), channel_id=1, replica_groups=mesh['req'=8,'head'=4] {'req'}, dimensions={0} | all-to-all | bytes 1048576 | tf_op jit(solution)/shard_map/all_to_all | solution.py:426
  44.5 1.5 collective-permute-start
  46.0 0.0 collective-permute-start.1
  46.0 10.8 %collective-permute-done.refs_1_ = bf16[128,2048]{1,0:T(8,128)(2,1)S(1)} collective-permute-done((bf16[128,2048]{1,0:T(8,128)(2,1)S(1)}, bf16[128,2048]{1,0:T(8,128)(2,1)S(1)}, u32[]{:S(2)}, u32[]{:S(2)}) %collective-permute-start) | collective-permute-done | bytes 524320 | tf_op jit(solution)/shard_map/ppermute | solution.py:419
  56.8 0.0 collective-permute-start.2
  56.8 0.5 collective-permute-start.4
  57.3 0.1 pad_add_fusion.scal
  57.4 0.0 collective-permute-done.1.refs_2_
  57.4 1.3 collective-permute-done.2.refs_3_
  58.7 5.5 %qkv.1 = (bf16[512,512]{1,0:T(8,128)(2,1)S(1)}, bf16[512,128]{1,0:T(8,128)(2,1)S(1)}, bf16[512,128]{1,0:T(8,128)(2,1)S(1)}) custom-call(bf16[128,2048]{1,0:T(8,128)(2,1)S(1)} %bitcast.29, bf16[128,2048]{1,0:T(8,128)(2,1)S(1)} %collective-permute-done.refs_1_, bf16[128,2048]{1,0:T(8,128)(2,1)S(1)} %collective-permute-done.1.refs_2_, ...), custom_call_target="tpu_custom_call" | custom-call | flops 1610612736 | bytes 5242880 | tf_op jit(solution)/shard_map/qkv/pallas_call | solution.py:132
  64.2 21.9 %attend_full.1 = bf16[512,512]{1,0:T(8,128)(2,1)S(1)} custom-call(s32[2]{0:T(128)S(1)} %pad_add_fusion.scal, bf16[512,512]{1,0:T(8,128)(2,1)S(1)} %get-tuple-element.21.q, bf16[2,4096,128]{2,1,0:T(8,128)(2,1)S(1)} %copy-done.10, bf16[2,4096,128]{2,1,0:T(8,128)(2,1)S(1)} %copy-done.12, bf16[512,128]{1,0:T(8,128)(2,1)S(1)} %get-tuple-element.24.refs_0_, ...), custom_call_target="tpu_custom_call" | custom-call | flops 19327352832 | bytes 4194304 | tf_op jit(solution)/shard_map/attend_full/pallas_call | solution.py:319
  86.1 0.2 collective-permute-start.3
  86.3 0.0 collective-permute-done.4.w_pair
  86.3 1.4 collective-permute-done.3.theirs
  87.7 2.2 %project.1 = (f32[128,2048]{1,0:T(8,128)S(1)}, bf16[128,2048]{1,0:T(8,128)(2,1)S(1)}) custom-call(bf16[256,512]{1,0:T(8,128)(2,1)S(1)} %get-tuple-element.29.mine, bf16[256,512]{1,0:T(8,128)(2,1)S(1)} %collective-permute-done.3.theirs, bf16[512,2048]{1,0:T(8,128)(2,1)S(1)} %copy-done, bf16[512,2048]{1,0:T(8,128)(2,1)S(1)} %collective-permute-done.4.w_pair), custom_call_target="tpu_custom_call" | custom-call | flops 1073741824 | bytes 6291456 | tf_op jit(solution)/shard_map/project/pallas_call | solution.py:399
  90.0 1.6 collective-permute-start.5
  91.6 12.5 %collective-permute-done.5 = bf16[128,2048]{1,0:T(8,128)(2,1)S(1)} collective-permute-done((bf16[128,2048]{1,0:T(8,128)(2,1)S(1)}, bf16[128,2048]{1,0:T(8,128)(2,1)S(1)}, u32[]{:S(2)}, u32[]{:S(2)}) %collective-permute-start.5) | collective-permute-done | bytes 524320 | tf_op jit(solution)/shard_map/ppermute | solution.py:419
  104.0 0.9 add_convert_fusion
  104.9 53.2 %all-to-all-start.2 = ((bf16[8,16,2048]{2,1,0:T(8,128)(2,1)}), bf16[8,16,2048]{2,1,0:T(8,128)(2,1)S(1)}, u32[]{:S(2)}, u32[]{:S(2)}) async-start(bf16[8,16,2048]{2,1,0:T(8,128)(2,1)} %bitcast.9), calls=%async_computation.2 | async-start | bytes 1048576 | tf_op jit(solution)/shard_map/all_to_all | solution.py:426
  158.1 0.1 select_reduce_fusion.order
  158.3 13.9 %all-to-all-done.2.x = bf16[8,16,2048]{2,1,0:T(8,128)(2,1)S(1)} async-done(((bf16[8,16,2048]{2,1,0:T(8,128)(2,1)}), bf16[8,16,2048]{2,1,0:T(8,128)(2,1)S(1)}, u32[]{:S(2)}, u32[]{:S(2)}) %all-to-all-start.2) | async-done | bytes 524320 | tf_op jit(solution)/shard_map/all_to_all | solution.py:426
  172.1 1.4 pick.1
  173.5 3.6 %all-to-all-start.3 = ((bf16[8,16,2048]{2,1,0:T(8,128)(2,1)}), bf16[8,16,2048]{2,1,0:T(8,128)(2,1)S(1)}, u32[]{:S(2)}, u32[]{:S(2)}) async-start(bf16[8,16,2048]{2,1,0:T(8,128)(2,1)} %pick.1), calls=%async_computation.3 | async-start | bytes 1048576 | tf_op jit(solution)/shard_map/all_to_all | solution.py:426
  177.2 0.6 gather_fusion
  177.8 0.6 gather_fusion.1
  178.4 0.8 bitcast_select_fusion
  179.2 12.3 %all-to-all-done.3 = bf16[8,16,2048]{2,1,0:T(8,128)(2,1)S(1)} async-done(((bf16[8,16,2048]{2,1,0:T(8,128)(2,1)}), bf16[8,16,2048]{2,1,0:T(8,128)(2,1)S(1)}, u32[]{:S(2)}, u32[]{:S(2)}) %all-to-all-start.3) | async-done | bytes 524320 | tf_op jit(solution)/shard_map/all_to_all | solution.py:426
  191.4 0.9 fusion
  (25 shorter events, 0.1 us)
Async XLA Ops:
  0.6 23.4 %all-to-all-start = ((bf16[8,16,2048]{2,1,0:T(8,128)(2,1)}), bf16[8,16,2048]{2,1,0:T(8,128)(2,1)S(1)}, u32[]{:S(2)}, u32[]{:S(2)}) async-start(bf16[8,16,2048]{2,1,0:T(8,128)(2,1)} %bitcast.37), calls=%async_computation | async-start | bytes 1048576 | tf_op jit(solution)/shard_map/all_to_all | solution.py:426
  7.9 4.3 %copy-start.1 = (f32[2048]{0:T(1024)S(1)}, f32[2048]{0:T(1024)}, u32[]{:S(2)}) copy-start(f32[2048]{0:T(1024)} %param.15) | copy-start | bytes 24580
  7.9 4.3 %copy-start.2 = (s32[1,384]{1,0:T(1,128)S(1)}, s32[1,384]{1,0:T(1,128)}, u32[]{:S(2)}) copy-start(s32[1,384]{1,0:T(1,128)} %index.1) | copy-start | bytes 4612
  7.9 4.3 %copy-start.4 = (bf16[1,384,2048]{2,1,0:T(8,128)(2,1)S(1)}, bf16[1,384,2048]{2,1,0:T(8,128)(2,1)}, u32[]{:S(2)}) copy-start(bf16[1,384,2048]{2,1,0:T(8,128)(2,1)} %param.22) | copy-start | bytes 4718596
  12.2 1.2 copy-start.5
  13.5 1.2 copy-start.6
  14.7 1.0 copy-start.7
  15.7 1.0 copy-start.8
  16.8 7.2 %copy-start.3 = (s32[8]{0:T(128)S(1)}, s32[8]{0:T(128)}, u32[]{:S(2)}) copy-start(s32[8]{0:T(128)} %order.1) | copy-start | bytes 100
  21.4 1.3 copy-start.9
  22.7 1.3 copy-start.11
  24.0 32.8 %copy-start = (bf16[512,2048]{1,0:T(8,128)(2,1)S(1)}, bf16[512,2048]{1,0:T(8,128)(2,1)}, u32[]{:S(2)}) copy-start(bf16[512,2048]{1,0:T(8,128)(2,1)} %w.1) | copy-start | bytes 6291460
  44.5 12.3 %collective-permute-start = (bf16[128,2048]{1,0:T(8,128)(2,1)S(1)}, bf16[128,2048]{1,0:T(8,128)(2,1)S(1)}, u32[]{:S(2)}, u32[]{:S(2)}) collective-permute-start(bf16[128,2048]{1,0:T(8,128)(2,1)S(1)} %bitcast.27), channel_id=1, source_target_pairs={{0,2},{1,3},{2,0},{3,1},{4,6},{5,7},{6,4},{7,5},{8,10},{9,11},{10,... | collective-permute-start | bytes 1572872 | tf_op jit(solution)/shard_map/ppermute | solution.py:419
  46.0 11.4 %collective-permute-start.1 = (bf16[128,2048]{1,0:T(8,128)(2,1)S(1)}, bf16[128,2048]{1,0:T(8,128)(2,1)S(1)}, u32[]{:S(2)}, u32[]{:S(2)}) collective-permute-start(bf16[128,2048]{1,0:T(8,128)(2,1)S(1)} %bitcast.28), channel_id=1, source_target_pairs={{0,1},{1,0},{2,3},{3,2},{4,5},{5,4},{6,7},{7,6},{8,9},{9,8},{10,11... | collective-permute-start | bytes 1572872 | tf_op jit(solution)/shard_map/ppermute | solution.py:419
  56.8 1.9 collective-permute-start.2
  56.8 29.6 %collective-permute-start.4 = (bf16[512,2048]{1,0:T(8,128)(2,1)S(1)}, bf16[512,2048]{1,0:T(8,128)(2,1)S(1)}, u32[]{:S(2)}, u32[]{:S(2)}) collective-permute-start(bf16[512,2048]{1,0:T(8,128)(2,1)S(1)} %copy-done), channel_id=1, source_target_pairs={{0,1},{1,0},{2,3},{3,2},{4,5},{5,4},{6,7},{7,6},{8,9},{9,8},{10,11... | collective-permute-start | bytes 6291464 | tf_op jit(solution)/shard_map/ppermute | solution.py:419
  57.4 6.8 %copy-start.10 = (bf16[2,4096,128]{2,1,0:T(8,128)(2,1)S(1)}, bf16[2,4096,128]{2,1,0:T(8,128)(2,1)}, u32[]{:S(2)}) copy-start(bf16[2,4096,128]{2,1,0:T(8,128)(2,1)} %copy-done.9) | copy-start | bytes 6291460
  57.4 6.8 %copy-start.12 = (bf16[2,4096,128]{2,1,0:T(8,128)(2,1)S(1)}, bf16[2,4096,128]{2,1,0:T(8,128)(2,1)}, u32[]{:S(2)}) copy-start(bf16[2,4096,128]{2,1,0:T(8,128)(2,1)} %copy-done.11) | copy-start | bytes 6291460
  86.1 1.6 collective-permute-start.3
  90.0 14.0 %collective-permute-start.5 = (bf16[128,2048]{1,0:T(8,128)(2,1)S(1)}, bf16[128,2048]{1,0:T(8,128)(2,1)S(1)}, u32[]{:S(2)}, u32[]{:S(2)}) collective-permute-start(bf16[128,2048]{1,0:T(8,128)(2,1)S(1)} %get-tuple-element.27), channel_id=1, source_target_pairs={{0,2},{1,3},{2,0},{3,1},{4,6},{5,7},{6,4},{7,5},{8,10},{9,11},{10,... | collective-permute-start | bytes 1572872 | tf_op jit(solution)/shard_map/ppermute | solution.py:419
  104.9 86.5 %copy-start.13 = (bf16[1,128,2048]{2,1,0:T(8,128)(2,1)S(1)}, bf16[1,128,2048]{2,1,0:T(8,128)(2,1)}, u32[]{:S(2)}) copy-start(bf16[1,128,2048]{2,1,0:T(8,128)(2,1)} %param.14) | copy-start | bytes 1572868
  104.9 67.2 %all-to-all-start.2 = ((bf16[8,16,2048]{2,1,0:T(8,128)(2,1)}), bf16[8,16,2048]{2,1,0:T(8,128)(2,1)S(1)}, u32[]{:S(2)}, u32[]{:S(2)}) async-start(bf16[8,16,2048]{2,1,0:T(8,128)(2,1)} %bitcast.9), calls=%async_computation.2 | async-start | bytes 1048576 | tf_op jit(solution)/shard_map/all_to_all | solution.py:426
  173.5 17.9 %all-to-all-start.3 = ((bf16[8,16,2048]{2,1,0:T(8,128)(2,1)}), bf16[8,16,2048]{2,1,0:T(8,128)(2,1)S(1)}, u32[]{:S(2)}, u32[]{:S(2)}) async-start(bf16[8,16,2048]{2,1,0:T(8,128)(2,1)} %pick.1), calls=%async_computation.3 | async-start | bytes 1048576 | tf_op jit(solution)/shard_map/all_to_all | solution.py:426

commit v3 on v2

--- a/solution.py
+++ b/solution.py
@@ -151,14 +151,15 @@
 
 KEYS = 1024
 ROWS = 1024
-CHUNKS = 1
-
-
-def att_kernel(portion, chunk, chunks, js, mode, scal, q, ka, va, *refs):
+PARTS = 2
+
+
+def att_kernel(chunks, js, mode, scal, q, ka, va, *refs):
     refs = list(refs)
     take_refs = lambda count: [refs.pop(0) for _ in range(count)]
     if mode != "cached":
         kn, vn = take_refs(chunks), take_refs(chunks)
+        (col,), row = take_refs(1), take_refs(chunks)
     if mode == "new":
         qa_in, acc_in = take_refs(2)
     if mode == "cached":
@@ -170,24 +171,15 @@
     if mode == "new":
         kbuf, vbuf = take_refs(2)
     tokens = q.shape[0]
-    length, head = scal[0], scal[1]
+    length = scal[0]
     per = q.shape[1] // HD // 2
     rows = per * tokens
     blocks = lax.div(length + (KEYS - 1), KEYS)
     lane = lane_of((tokens, LANES))
     spans = [slice(g * tokens, (g + 1) * tokens) for g in range(per)]
 
-    def token(i, part):
-        which = lax.div(i, portion)
-        swapped = which if mode is None else lax.div(which, 2) + 2 * lax.rem(which, 2)
-        return (swapped ^ head) * (portion * chunks) + part * portion + (i - which * portion)
-
     if mode != "cached":
-        own = token(lax.broadcasted_iota(jnp.int32, (tokens, tokens), 0), chunk)
-        allowed = [
-            token(lax.broadcasted_iota(jnp.int32, (tokens, tokens), 1), part) <= own
-            for part in range(chunks)
-        ]
+        allowed = [jnp.broadcast_to(x[...], (tokens, tokens)) <= col[...] for x in row]
 
     for n, j in enumerate(js):
         if mode == "cached":
@@ -292,8 +284,8 @@
             o[:, at] = jnp.where(lane < HD, pair[0], pltpu.roll(pair[1], HD, 1)).astype(BF16)
 
 
-def attend(portion, chunk, js, mode, scal, q, ka, va, kns=(), vns=(), began=()):
-    tokens, chunks = q.shape[0], CHUNKS
+def attend(js, mode, scal, q, ka, va, kns=(), vns=(), places=(), began=()):
+    tokens, chunks = q.shape[0], PARTS
     rows = q.shape[1] // HD // 2 * tokens
     keys = {"cached": ka.shape[1], "new": tokens * chunks, "full": ka.shape[1] + tokens * chunks}[mode]
     scratch = []
@@ -317,9 +309,9 @@
         out = jax.ShapeDtypeStruct((tokens, q.shape[1] // 2 * len(js)), BF16)
         specs = VM
     return pl.pallas_call(
-        functools.partial(att_kernel, portion, chunk, chunks, js, mode),
+        functools.partial(att_kernel, chunks, js, mode),
         out_shape=out,
-        in_specs=[SM, VM, cached, cached] + [VM] * (len(kns) + len(vns) + len(began)),
+        in_specs=[SM, VM, cached, cached] + [VM] * (len(kns) + len(vns) + len(places) + len(began)),
         out_specs=specs,
         scratch_shapes=scratch,
         compiler_params=pltpu.CompilerParams(vmem_limit_bytes=32 << 20),
@@ -329,7 +321,7 @@
             transcendentals=rows * len(js) * keys,
         ),
         name="attend_" + mode,
-    )(scal, q, ka, va, *kns, *vns, *began)
+    )(scal, q, ka, va, *kns, *vns, *places, *began)
 
 
 def tables(positions):
@@ -380,32 +372,25 @@
     )(order, x, gain)
 
 
-def project_kernel(mine, theirs, w, w_pair, keep, send):
+def project_kernel(mine, theirs, w, w_pair, out):
     terms = [
         jnp.dot(x[...], y[...], preferred_element_type=F32).astype(BF16).astype(F32)
         for x, y in ((mine, w), (theirs, w_pair))
     ]
-    total = terms[0] + terms[1]
-    half = keep.shape[0]
-    keep[...] = total[:half]
-    send[...] = total[half:].astype(BF16)
-
-
-def project(mine, theirs, w, w_pair):
+    out[...] = (terms[0] + terms[1]).astype(out.dtype)
+
+
+def project(mine, theirs, w, w_pair, kind):
     rows, depth = mine.shape
     width = w.shape[1]
     step = 512
-    half = rows // 2
     return pl.pallas_call(
         project_kernel,
-        out_shape=(
-            jax.ShapeDtypeStruct((half, width), F32),
-            jax.ShapeDtypeStruct((half, width), BF16),
-        ),
+        out_shape=jax.ShapeDtypeStruct((rows, width), kind),
         grid=(width // step,),
         in_specs=[pl.BlockSpec((rows, depth), lambda n: (0, 0))] * 2
         + [pl.BlockSpec((depth, step), lambda n: (0, n))] * 2,
-        out_specs=(pl.BlockSpec((half, step), lambda n: (0, n)),) * 2,
+        out_specs=pl.BlockSpec((rows, step), lambda n: (0, n)),
         compiler_params=pltpu.CompilerParams(vmem_limit_bytes=16 << 20),
         cost_estimate=pl.CostEstimate(
             flops=4 * rows * depth * width, bytes_accessed=6 << 20, transcendentals=0
@@ -444,43 +429,27 @@
     assert requests_here == 1
     heads = lax.axis_size("head")
     head = lax.axis_index("head")
-    portion = positions_here // CHUNKS
     mine = hidden_in[0]
     gain = norm_gain[None, :]
     length = cache_lengths[0]
-    relative = jnp.arange(heads).reshape(2, heads // 2).T.reshape(-1) ^ head
-    tables_of = [
-        tables(
-            (
-                relative[:, None] * positions_here + part * portion + jnp.arange(portion)[None, :]
-            ).reshape(-1).astype(F32)
-            + length.astype(F32)
-        )
-        for part in range(CHUNKS)
-    ]
-    scal = jnp.stack([length, head.astype(jnp.int32)])
     tie = lax.optimization_barrier
-    flat = lambda x: x.reshape(portion, features)
+    flat = lambda x: x.reshape(positions_here, features)
     far_bit, near_bit = heads // 2, 1
+    inner = jnp.arange(positions_here)
+    place = lambda bits: jnp.concatenate(
+        [(head ^ bit) * positions_here + inner for bit in bits]
+    ).astype(jnp.int32)
+    here, there = place((0, near_bit)), place((far_bit, far_bit + near_bit))
+    new_tables = [tables(length.astype(F32) + x.astype(F32)) for x in (here, there)]
+    rows_of = [here[None, :], there[None, :]]
+    held_cos, held_sin = tables(recompute_index[0].astype(F32))
     w_pair = swap(output_weight, "head", near_bit)
-    held_cos, held_sin = tables(recompute_index[0].astype(F32))
-
-    def project_in(c, own):
-        far = swap(own, "head", far_bit)
-        near = swap(own, "head", near_bit)
-        corner = swap(far, "head", near_bit)
-        return qkv([own, far, near, corner], query_weight, key_weight, value_weight, *tables_of[c])
-
-    def project_out(pieces):
-        attended = pieces[0] if len(pieces) == 1 else jnp.concatenate(pieces, axis=1)
-        theirs = swap(attended[2 * portion :], "head", near_bit)
-        keep, send = project(attended[: 2 * portion], theirs, output_weight, w_pair)
-        return keep, swap(send, "head", far_bit)
-
-    join = lambda keep, got: (keep + got.astype(F32)).astype(BF16)
     slots = jnp.arange(slot_request.shape[0], dtype=jnp.int32)
     inverse = jnp.sum(jnp.where(slot_request[None, :] == slots[:, None], slots[None, :], 0), axis=1)
 
+    first = spread(mine)
+    first, new_tables, held_cos, held_sin = tie((first, new_tables, held_cos, held_sin))
+    own = flat(spread(flat(pick_norm(first, slot_request, gain))))
     ka, va = prep(
         cache_lengths,
         held_states[0],
@@ -493,22 +462,38 @@
         cache_keys[0],
         cache_values[0],
     )
-    first = spread(mine)
-    first, ka, va, tables_of = tie((first, ka, va, tables_of))
-    own = flat(spread(flat(pick_norm(first, slot_request, gain))))
-    q, kn, vn = project_in(0, own)
-    kns, vns = [kn], [vn]
-    attended = attend(portion, 0, (0, 1), "full", scal, q, ka, va, kns, vns)
-    back = spread(join(*project_out([attended])))
-    returned = [flat(spread(flat(pick(back, inverse))))]
-    returned = jnp.concatenate(returned, axis=0)
+    own, ka, va = tie((own, ka, va))
+
+    far = swap(own, "head", far_bit)
+    near = swap(own, "head", near_bit)
+    weights = (query_weight, key_weight, value_weight)
+    q_here, kn_here, vn_here = qkv([own, near], *weights, *new_tables[0])
+    began = attend((0,), "cached", cache_lengths, q_here, ka, va)
+    far, began = tie((far, began))
+    corner = swap(far, "head", near_bit)
+    q_there, kn_there, vn_there = qkv([far, corner], *weights, *new_tables[1])
+    kns, vns = [kn_here, kn_there], [vn_here, vn_there]
+
+    def turn_over(attended, kind):
+        theirs = swap(attended[positions_here:], "head", near_bit)
+        return project(attended[:positions_here], theirs, output_weight, w_pair, kind)
+
+    args = (cache_lengths, q_there, ka, va, kns, vns, [there[:, None], *rows_of])
+    sent = turn_over(attend((0, 1), "full", *args), BF16)
+    sent, q_here = tie((sent, q_here))
+    args = (cache_lengths, q_here, ka, va, kns, vns, [here[:, None], *rows_of])
+    halves = [attend((0,), "new", *args, began), attend((1,), "full", *args)]
+    kept = turn_over(jnp.concatenate(halves, axis=1), F32)
+    got = swap(sent, "head", far_bit)
+    back = spread((kept + got.astype(F32)).astype(BF16))
+    returned = flat(spread(flat(pick(back, inverse))))
     hidden_out = (mine.astype(F32) + returned.astype(F32)).astype(BF16)
 
     away = jnp.arange(heads) ^ head
 
     def by_token(pieces):
-        stacked = jnp.stack([x.reshape(heads, portion, LANES) for x in pieces], axis=1)
-        return jnp.take(stacked, lax.div(away, 2) + 2 * lax.rem(away, 2), axis=0).reshape(1, heads * positions_here, LANES)
+        joined = jnp.concatenate(pieces, axis=0).reshape(heads, positions_here, LANES)
+        return jnp.take(joined, away, axis=0).reshape(1, heads * positions_here, LANES)
 
     return (hidden_out[None], by_token(kns), by_token(vns))
 

time: 193 us -> 208 us (1.078)
  Pallas kernels: 36.3 us -> 120 us
  starting transfers between devices: 67.9 us -> 22.3 us
  blocking collectives: 19.7 us -> 0 us
  waiting for transfers between devices: 52.1 us -> 40.6 us
  local copies, waits for them, and re-layouts: 8.46 us -> 14.9 us
    pallas_call x2 -> x6, Pallas kernels: 24.1 us -> 106 us  [the longest x4 99.1 us: attend(): pl.pallas_call(functools.partial(att_kernel, chunks, js, mode), out_shape...]
    all_to_all x3 -> x4, starting transfers between devices: 64.1 us -> 18.5 us  [spread(): lax.all_to_all(pieces, 'req', split_axis=0, concat_axis=0, tiled=True)]
    ppermute x6 -> x7, waiting for transfers between devices: 25.9 us -> 3.67 us  [swap(): return lax.ppermute(x, axis, [(i, i ^ bits) for i in range(size)])]
    all_to_all x1 -> x0, blocking collectives: 19.7 us -> none  [spread(): lax.all_to_all(pieces, 'req', split_axis=0, concat_axis=0, tiled=True)]
    all_to_all x3 -> x4, waiting for transfers between devices: 26.1 us -> 36.9 us  [spread(): lax.all_to_all(pieces, 'req', split_axis=0, concat_axis=0, tiled=True)]
    unnamed x28 -> x88, local copies, waits for them, and re-layouts: 7.19 us -> 12.8 us
    pallas_call x1 -> x2, Pallas kernels: 5.49 us -> 6.48 us  [qkv(): pl.pallas_call(functools.partial(qkv_kernel, len(xs)), out_shape=(out(wid...]
  transfers between devices with their start and end apart: 9 -> 11, of which waited for: 6 -> 9; matrix products, arithmetic and copies ran while one was open for 3% -> 4% of each run, Pallas kernels for 17% -> 55%
where the time goes in v3:
time: 208 us; the launch traced here: 207 us
  Pallas kernels  120 us (58%)
  waiting for transfers between devices  40.6 us (20%)
  starting transfers between devices  22.3 us (11%)
  local copies, waits for them, and re-layouts  14.9 us (7%)
  other arithmetic  7.77 us (4%)
    pallas_call x4, Pallas kernels, attend(): pl.pallas_call(functools.partial(att_kernel, chunks, js, mode), out_shape...  99.1 us
    all_to_all x4, waiting for transfers between devices, spread(): lax.all_to_all(pieces, 'req', split_axis=0, concat_axis=0, tiled=True)  36.9 us
    all_to_all x4, starting transfers between devices, spread(): lax.all_to_all(pieces, 'req', split_axis=0, concat_axis=0, tiled=True)  18.5 us
    unnamed x88, local copies, waits for them, and re-layouts  12.8 us
    pallas_call x2, Pallas kernels, project(): pl.pallas_call(project_kernel, out_shape=jax.ShapeDtypeStruct((rows, widt...  6.65 us
    pallas_call x2, Pallas kernels, qkv(): pl.pallas_call(functools.partial(qkv_kernel, len(xs)), out_shape=(out(wid...  6.48 us
    pallas_call x1, Pallas kernels, prep(): pl.pallas_call(prep_kernel, out_shape=(out, out), in_specs=[SM] + [VM] *...  4.57 us
  transfers between devices with their start and end apart: 11, of which 9 were waited for; matrix products, arithmetic and copies ran while one was open for 4% of the time, Pallas kernels for 55%

profile of v3, /device:TPU:0, one launch (start us, length us, event | category | flops | bytes accessed | tf_op | source)
XLA Modules:
  0.0 207.2 jit_solution(10703854624219400190)
XLA Ops:
  0.6 7.3 %all-to-all-start = ((bf16[8,16,2048]{2,1,0:T(8,128)(2,1)}), bf16[8,16,2048]{2,1,0:T(8,128)(2,1)S(1)}, u32[]{:S(2)}, u32[]{:S(2)}) async-start(bf16[8,16,2048]{2,1,0:T(8,128)(2,1)} %bitcast.33), calls=%async_computation | async-start | bytes 1048576 | tf_op jit(solution)/shard_map/all_to_all | solution.py:411
  8.7 0.4 copy-done.36
  9.2 1.0 fusion.4
  10.2 0.7 convert_reduce_fusion
  10.9 0.8 pad_maximum_fusion.3.refs_5_
  12.3 0.8 fusion.2
  13.1 1.1 pad_maximum_fusion
  14.2 8.2 %all-to-all-done.x = bf16[8,16,2048]{2,1,0:T(8,128)(2,1)S(1)} async-done(((bf16[8,16,2048]{2,1,0:T(8,128)(2,1)}), bf16[8,16,2048]{2,1,0:T(8,128)(2,1)S(1)}, u32[]{:S(2)}, u32[]{:S(2)}) %all-to-all-start) | async-done | bytes 524320 | tf_op jit(solution)/shard_map/all_to_all | solution.py:411
  22.4 1.6 pick_norm.1
  23.9 4.2 %all-to-all-start.1 = ((bf16[8,16,2048]{2,1,0:T(8,128)(2,1)}), bf16[8,16,2048]{2,1,0:T(8,128)(2,1)}, u32[]{:S(2)}, u32[]{:S(2)}) async-start(bf16[8,16,2048]{2,1,0:T(8,128)(2,1)} %pick_norm.1), calls=%async_computation.1 | async-start | bytes 1048576 | tf_op jit(solution)/shard_map/all_to_all | solution.py:411
  28.1 0.9 copy-done.26
  29.1 0.9 copy-done.27
  30.0 1.4 copy-done.32
  31.4 1.2 copy-done.33
  32.6 1.2 copy-done.34
  33.9 4.6 %prep.1 = (bf16[2,4096,128]{2,1,0:T(8,128)(2,1)S(1)}, bf16[2,4096,128]{2,1,0:T(8,128)(2,1)S(1)}) custom-call(s32[1]{0:T(128)S(6)} %copy.27.length.scal, bf16[384,2048]{1,0:T(8,128)(2,1)S(1)} %bitcast.30, f32[1,2048]{1,0:T(1,128)S(1)} %bitcast.29, bf16[2048,128]{1,0:T(8,128)(2,1)S(1)} %copy-done.1, bf16[2048,128]{1,0:T(8,128)(2,1)S(1)} %copy-done.2, ...), custom_call_target="tpu_custom_call" | custom-call | flops 3000000000 | bytes 8388608 | tf_op jit(solution)/shard_map/prep/pallas_call | solution.py:88
  38.4 1.4 copy-done.3
  39.8 1.4 copy-done.7
  41.2 1.2 all-to-all-done.1
  42.4 1.6 collective-permute-start
  44.5 0.9 copy-done.11
  45.4 3.2 %qkv.2 = (bf16[256,512]{1,0:T(8,128)(2,1)S(1)}, bf16[256,128]{1,0:T(8,128)(2,1)S(1)}, bf16[256,128]{1,0:T(8,128)(2,1)S(1)}) custom-call(bf16[128,2048]{1,0:T(8,128)(2,1)} %bitcast.3.refs_0_, bf16[128,2048]{1,0:T(8,128)(2,1)S(1)} %collective-permute-done.1.refs_1_, bf16[2048,512]{1,0:T(8,128)(2,1)} %refs_2_.3, bf16[2048,128]{1,0:T(8,128)(2,1)} %refs_3_.3, ...), custom_call_target="tpu_custom_call" | custom-call | flops 805306368 | bytes 5242880 | tf_op jit(solution)/shard_map/qkv/pallas_call | solution.py:132
  48.6 0.6 copy-done.14
  49.2 0.6 copy-done.16
  49.9 5.4 %attend_cached.1 = (bf16[1,1024,128]{2,1,0:T(8,128)(2,1)S(1)}, f32[1,1024,128]{2,1,0:T(8,128)S(1)}) custom-call(s32[1]{0:T(128)S(6)} %copy.27.length.scal, bf16[256,512]{1,0:T(8,128)(2,1)S(1)} %get-tuple-element.50.q, bf16[2,4096,128]{2,1,0:T(8,128)(2,1)S(1)} %copy-done.4, bf16[2,4096,128]{2,1,0:T(8,128)(2,1)S(1)} %copy-done.8), custom_call_target="tpu_custom_call" | custom-call | flops 4294967296 | bytes 4194304 | tf_op jit(solution)/shard_map/attend_cached/pallas_call | solution.py:311
  55.4 0.8 copy-done.12
  56.2 0.7 copy-done.24
  57.0 0.8 copy.24.refs_4_
  57.9 0.9 collective-permute-done.2.refs_1_
  58.9 3.3 %qkv.3 = (bf16[256,512]{1,0:T(8,128)(2,1)S(1)}, bf16[256,128]{1,0:T(8,128)(2,1)S(1)}, bf16[256,128]{1,0:T(8,128)(2,1)S(1)}) custom-call(bf16[128,2048]{1,0:T(8,128)(2,1)S(1)} %collective-permute-done.refs_0_, bf16[128,2048]{1,0:T(8,128)(2,1)S(1)} %collective-permute-done.2.refs_1_, bf16[2048,512]{1,0:T(8,128)(2,1)} %refs_2_.3, bf16[2048,128]{1,0:T(8,128)(2,1)} %refs_3_.3, ...), custom_call_target="tpu_custom_call" | custom-call | flops 805306368 | bytes 5242880 | tf_op jit(solution)/shard_map/qkv/pallas_call | solution.py:132
  62.3 49.5 %attend_full.2 = bf16[256,512]{1,0:T(8,128)(2,1)S(1)} custom-call(s32[1]{0:T(128)S(6)} %copy.27.length.scal, bf16[256,512]{1,0:T(8,128)(2,1)S(1)} %get-tuple-element.45.q, bf16[2,4096,128]{2,1,0:T(8,128)(2,1)S(1)} %copy-done.5, bf16[2,4096,128]{2,1,0:T(8,128)(2,1)S(1)} %copy-done.9, bf16[256,128]{1,0:T(8,128)(2,1)S(1)} %copy-done.15, ...), custom_call_target="tpu_custom_call" | custom-call | flops 9663676416 | bytes 4194304 | tf_op jit(solution)/shard_map/attend_full/pallas_call | solution.py:311
  112.3 0.9 collective-permute-done.3.theirs
  113.3 3.4 %project.2 = bf16[128,2048]{1,0:T(8,128)(2,1)S(1)} custom-call(bf16[128,512]{1,0:T(8,128)(2,1)S(1)} %get-tuple-element.57.mine, bf16[128,512]{1,0:T(8,128)(2,1)S(1)} %collective-permute-done.3.theirs, bf16[512,2048]{1,0:T(8,128)(2,1)S(1)} %copy-done, bf16[512,2048]{1,0:T(8,128)(2,1)} %collective-permute-done.4.w_pair), custom_call_target="tpu_custom_call" | custom-call | flops 536870912 | bytes 6291456 | tf_op jit(solution)/shard_map/project/pallas_call | solution.py:387
  116.7 1.6 collective-permute-start.6
  118.3 24.9 %attend_full.3 = bf16[256,256]{1,0:T(8,128)(2,1)S(1)} custom-call(s32[1]{0:T(128)S(6)} %copy.27.length.scal, bf16[256,512]{1,0:T(8,128)(2,1)S(1)} %copy-done.23, bf16[2,4096,128]{2,1,0:T(8,128)(2,1)S(1)} %copy-done.6, bf16[2,4096,128]{2,1,0:T(8,128)(2,1)S(1)} %copy-done.10, bf16[256,128]{1,0:T(8,128)(2,1)S(1)} %copy-done.15, ...), custom_call_target="tpu_custom_call" | custom-call | flops 4831838208 | bytes 4194304 | tf_op jit(solution)/shard_map/attend_full/pallas_call | solution.py:311
  143.2 19.2 %attend_new.1 = bf16[256,256]{1,0:T(8,128)(2,1)S(1)} custom-call(s32[1]{0:T(128)S(6)} %copy.27.length.scal, bf16[256,512]{1,0:T(8,128)(2,1)S(1)} %copy-done.23, bf16[2,4096,128]{2,1,0:T(8,128)(2,1)S(1)} %copy-done.6, bf16[2,4096,128]{2,1,0:T(8,128)(2,1)S(1)} %copy-done.10, bf16[256,128]{1,0:T(8,128)(2,1)S(1)} %copy-done.15, bf16[256,128]{1,0:T(8,128)(2,1)S(1)} %copy-done.19, ...), custom_call_target="tpu_custom_call" | custom-call | flops 536870912 | bytes 4194304 | tf_op jit(solution)/shard_map/attend_new/pallas_call | solution.py:311
  162.6 1.3 collective-permute-done.5.theirs
  163.9 3.3 %project.3 = f32[128,2048]{1,0:T(8,128)S(1)} custom-call(bf16[128,512]{1,0:T(8,128)(2,1)S(1)} %get-tuple-element.55.mine, bf16[128,512]{1,0:T(8,128)(2,1)S(1)} %collective-permute-done.5.theirs, bf16[512,2048]{1,0:T(8,128)(2,1)S(1)} %copy-done, bf16[512,2048]{1,0:T(8,128)(2,1)} %collective-permute-done.4.w_pair), custom_call_target="tpu_custom_call" | custom-call | flops 536870912 | bytes 6291456 | tf_op jit(solution)/shard_map/project/pallas_call | solution.py:387
  167.2 0.9 add_convert_fusion
  168.1 3.5 %all-to-all-start.2 = ((bf16[8,16,2048]{2,1,0:T(8,128)(2,1)}), bf16[8,16,2048]{2,1,0:T(8,128)(2,1)S(1)}, u32[]{:S(2)}, u32[]{:S(2)}) async-start(bf16[8,16,2048]{2,1,0:T(8,128)(2,1)} %bitcast.11), calls=%async_computation.2 | async-start | bytes 1048576 | tf_op jit(solution)/shard_map/all_to_all | solution.py:411
  171.7 14.9 %all-to-all-done.2.x = bf16[8,16,2048]{2,1,0:T(8,128)(2,1)S(1)} async-done(((bf16[8,16,2048]{2,1,0:T(8,128)(2,1)}), bf16[8,16,2048]{2,1,0:T(8,128)(2,1)S(1)}, u32[]{:S(2)}, u32[]{:S(2)}) %all-to-all-start.2) | async-done | bytes 524320 | tf_op jit(solution)/shard_map/all_to_all | solution.py:411
  186.6 1.4 pick.1
  188.0 3.6 %all-to-all-start.3 = ((bf16[8,16,2048]{2,1,0:T(8,128)(2,1)}), bf16[8,16,2048]{2,1,0:T(8,128)(2,1)S(1)}, u32[]{:S(2)}, u32[]{:S(2)}) async-start(bf16[8,16,2048]{2,1,0:T(8,128)(2,1)} %pick.1), calls=%async_computation.3 | async-start | bytes 1048576 | tf_op jit(solution)/shard_map/all_to_all | solution.py:411
  191.7 0.6 gather_fusion.1
  192.3 0.6 gather_fusion
  192.9 0.8 broadcast_select_fusion
  193.7 12.7 %all-to-all-done.3 = bf16[8,16,2048]{2,1,0:T(8,128)(2,1)S(1)} async-done(((bf16[8,16,2048]{2,1,0:T(8,128)(2,1)}), bf16[8,16,2048]{2,1,0:T(8,128)(2,1)S(1)}, u32[]{:S(2)}, u32[]{:S(2)}) %all-to-all-start.3) | async-done | bytes 524320 | tf_op jit(solution)/shard_map/all_to_all | solution.py:411
  206.3 0.9 fusion
  (104 shorter events, 2.2 us)
Async XLA Ops:
  0.6 21.8 %all-to-all-start = ((bf16[8,16,2048]{2,1,0:T(8,128)(2,1)}), bf16[8,16,2048]{2,1,0:T(8,128)(2,1)S(1)}, u32[]{:S(2)}, u32[]{:S(2)}) async-start(bf16[8,16,2048]{2,1,0:T(8,128)(2,1)} %bitcast.33), calls=%async_computation | async-start | bytes 1048576 | tf_op jit(solution)/shard_map/all_to_all | solution.py:411
  7.9 14.5 %copy-start.29 = (f32[2048]{0:T(1024)S(1)}, f32[2048]{0:T(1024)}, u32[]{:S(2)}) copy-start(f32[2048]{0:T(1024)} %param.15) | copy-start | bytes 24580
  7.9 14.5 %copy-start.31 = (s32[8]{0:T(128)S(1)}, s32[8]{0:T(128)}, u32[]{:S(2)}) copy-start(s32[8]{0:T(128)} %order.1) | copy-start | bytes 100
  12.1 16.0 %copy-start.1 = (bf16[2048,128]{1,0:T(8,128)(2,1)S(1)}, bf16[2048,128]{1,0:T(8,128)(2,1)}, u32[]{:S(2)}) copy-start(bf16[2048,128]{1,0:T(8,128)(2,1)} %refs_3_.3) | copy-start | bytes 1572868
  12.1 16.0 %copy-start.2 = (bf16[2048,128]{1,0:T(8,128)(2,1)S(1)}, bf16[2048,128]{1,0:T(8,128)(2,1)}, u32[]{:S(2)}) copy-start(bf16[2048,128]{1,0:T(8,128)(2,1)} %refs_4_.3) | copy-start | bytes 1572868
  12.1 16.0 %copy-start.30 = (s32[1,384]{1,0:T(1,128)S(1)}, s32[1,384]{1,0:T(1,128)}, u32[]{:S(2)}) copy-start(s32[1,384]{1,0:T(1,128)} %index.1) | copy-start | bytes 4612
  23.9 18.5 %all-to-all-start.1 = ((bf16[8,16,2048]{2,1,0:T(8,128)(2,1)}), bf16[8,16,2048]{2,1,0:T(8,128)(2,1)}, u32[]{:S(2)}, u32[]{:S(2)}) async-start(bf16[8,16,2048]{2,1,0:T(8,128)(2,1)} %pick_norm.1), calls=%async_computation.1 | async-start | bytes 1048576 | tf_op jit(solution)/shard_map/all_to_all | solution.py:411
  28.1 0.9 copy-start.26
  29.1 0.9 copy-start.27
  30.0 1.4 copy-start.32
  31.4 1.2 copy-start.33
  32.6 1.2 copy-start.34
  33.9 10.1 %copy-start = (bf16[512,2048]{1,0:T(8,128)(2,1)S(1)}, bf16[512,2048]{1,0:T(8,128)(2,1)}, u32[]{:S(2)}) copy-start(bf16[512,2048]{1,0:T(8,128)(2,1)} %w.3) | copy-start | bytes 6291460
  38.4 1.4 copy-start.3
  39.8 1.4 copy-start.7
  42.4 7.5 %copy-start.4 = (bf16[2,4096,128]{2,1,0:T(8,128)(2,1)S(1)}, bf16[2,4096,128]{2,1,0:T(8,128)(2,1)}, u32[]{:S(2)}) copy-start(bf16[2,4096,128]{2,1,0:T(8,128)(2,1)} %copy-done.3) | copy-start | bytes 6291460
  42.4 7.5 %copy-start.8 = (bf16[2,4096,128]{2,1,0:T(8,128)(2,1)S(1)}, bf16[2,4096,128]{2,1,0:T(8,128)(2,1)}, u32[]{:S(2)}) copy-start(bf16[2,4096,128]{2,1,0:T(8,128)(2,1)} %copy-done.7) | copy-start | bytes 6291460
  42.4 2.1 %collective-permute-start.1 = (bf16[128,2048]{1,0:T(8,128)(2,1)}, bf16[128,2048]{1,0:T(8,128)(2,1)S(1)}, u32[]{:S(2)}, u32[]{:S(2)}) collective-permute-start(bf16[128,2048]{1,0:T(8,128)(2,1)} %bitcast.3.refs_0_), channel_id=1, source_target_pairs={{0,1},{1,0},{2,3},{3,2},{4,5},{5,4},{6,7},{7,6},{8,9},{9,8},{10,11... | collective-permute-start | bytes 1572872 | tf_op jit(solution)/shard_map/ppermute | solution.py:404
  42.4 14.5 %collective-permute-start = (bf16[128,2048]{1,0:T(8,128)(2,1)}, bf16[128,2048]{1,0:T(8,128)(2,1)S(1)}, u32[]{:S(2)}, u32[]{:S(2)}) collective-permute-start(bf16[128,2048]{1,0:T(8,128)(2,1)} %bitcast.3.refs_0_), channel_id=1, source_target_pairs={{0,2},{1,3},{2,0},{3,1},{4,6},{5,7},{6,4},{7,5},{8,10},{9,11},{10,... | collective-permute-start | bytes 1572872 | tf_op jit(solution)/shard_map/ppermute | solution.py:404
  44.0 68.3 %collective-permute-start.4 = (bf16[512,2048]{1,0:T(8,128)(2,1)S(1)}, bf16[512,2048]{1,0:T(8,128)(2,1)}, u32[]{:S(2)}, u32[]{:S(2)}) collective-permute-start(bf16[512,2048]{1,0:T(8,128)(2,1)S(1)} %copy-done), channel_id=1, source_target_pairs={{0,1},{1,0},{2,3},{3,2},{4,5},{5,4},{6,7},{7,6},{8,9},{9,8},{10,11... | collective-permute-start | bytes 6291464 | tf_op jit(solution)/shard_map/ppermute | solution.py:404
  44.5 0.9 copy-start.11
  49.9 5.5 %copy-start.22 = (bf16[256,512]{1,0:T(8,128)(2,1)}, bf16[256,512]{1,0:T(8,128)(2,1)S(1)}, u32[]{:S(2)}) copy-start(bf16[256,512]{1,0:T(8,128)(2,1)S(1)} %get-tuple-element.50.q) | copy-start | bytes 786436
  49.9 7.2 %copy-start.37 = (s32[128]{0:T(128)S(1)}, s32[128]{0:T(128)}, u32[]{:S(2)}) copy-start(s32[128]{0:T(128)} %copy-done.36) | copy-start | bytes 1540
  49.9 7.2 %copy-start.39 = (s32[128]{0:T(128)S(1)}, s32[128]{0:T(128)}, u32[]{:S(2)}) copy-start(s32[128]{0:T(128)} %copy-done.38) | copy-start | bytes 1540
  49.9 8.0 %copy-start.41 = (s32[128]{0:T(128)S(1)}, s32[128]{0:T(128)}, u32[]{:S(2)}) copy-start(s32[128]{0:T(128)} %copy-done.40) | copy-start | bytes 1540
  49.9 8.0 %copy-start.43 = (s32[128]{0:T(128)S(1)}, s32[128]{0:T(128)}, u32[]{:S(2)}) copy-start(s32[128]{0:T(128)} %copy-done.42) | copy-start | bytes 1540
  55.4 0.8 copy-start.12
  57.0 1.9 collective-permute-start.2
  57.9 4.4 %copy-start.5 = (bf16[2,4096,128]{2,1,0:T(8,128)(2,1)S(1)}, bf16[2,4096,128]{2,1,0:T(8,128)(2,1)}, u32[]{:S(2)}) copy-start(bf16[2,4096,128]{2,1,0:T(8,128)(2,1)} %copy-done.3) | copy-start | bytes 6291460
  57.9 4.4 %copy-start.9 = (bf16[2,4096,128]{2,1,0:T(8,128)(2,1)S(1)}, bf16[2,4096,128]{2,1,0:T(8,128)(2,1)}, u32[]{:S(2)}) copy-start(bf16[2,4096,128]{2,1,0:T(8,128)(2,1)} %copy-done.7) | copy-start | bytes 6291460
  57.9 4.4 %copy-start.15 = (bf16[256,128]{1,0:T(8,128)(2,1)S(1)}, bf16[256,128]{1,0:T(8,128)(2,1)}, u32[]{:S(2)}) copy-start(bf16[256,128]{1,0:T(8,128)(2,1)} %copy-done.14) | copy-start | bytes 196612
  57.9 4.4 %copy-start.17 = (bf16[256,128]{1,0:T(8,128)(2,1)S(1)}, bf16[256,128]{1,0:T(8,128)(2,1)}, u32[]{:S(2)}) copy-start(bf16[256,128]{1,0:T(8,128)(2,1)} %copy-done.16) | copy-start | bytes 196612
  57.9 4.4 %copy-start.28 = (s32[256,1]{1,0:T(8,128)S(1)}, s32[256,1]{1,0:T(8,128)}, u32[]{:S(2)}) copy-start(s32[256,1]{1,0:T(8,128)} %copy.24.refs_4_) | copy-start | bytes 3076
  62.2 49.6 %copy-start.18 = (bf16[256,128]{1,0:T(8,128)(2,1)}, bf16[256,128]{1,0:T(8,128)(2,1)S(1)}, u32[]{:S(2)}) copy-start(bf16[256,128]{1,0:T(8,128)(2,1)S(1)} %get-tuple-element.47.refs_1_) | copy-start | bytes 196612
  62.2 49.6 %copy-start.20 = (bf16[256,128]{1,0:T(8,128)(2,1)}, bf16[256,128]{1,0:T(8,128)(2,1)S(1)}, u32[]{:S(2)}) copy-start(bf16[256,128]{1,0:T(8,128)(2,1)S(1)} %get-tuple-element.49.refs_3_) | copy-start | bytes 196612
  111.9 1.4 collective-permute-start.3
  113.3 5.0 %copy-start.6 = (bf16[2,4096,128]{2,1,0:T(8,128)(2,1)S(1)}, bf16[2,4096,128]{2,1,0:T(8,128)(2,1)}, u32[]{:S(2)}) copy-start(bf16[2,4096,128]{2,1,0:T(8,128)(2,1)} %copy-done.3) | copy-start | bytes 6291460
  113.3 5.0 %copy-start.10 = (bf16[2,4096,128]{2,1,0:T(8,128)(2,1)S(1)}, bf16[2,4096,128]{2,1,0:T(8,128)(2,1)}, u32[]{:S(2)}) copy-start(bf16[2,4096,128]{2,1,0:T(8,128)(2,1)} %copy-done.7) | copy-start | bytes 6291460
  113.3 5.0 %copy-start.19 = (bf16[256,128]{1,0:T(8,128)(2,1)S(1)}, bf16[256,128]{1,0:T(8,128)(2,1)}, u32[]{:S(2)}) copy-start(bf16[256,128]{1,0:T(8,128)(2,1)} %copy-done.18) | copy-start | bytes 196612
  113.3 5.0 %copy-start.21 = (bf16[256,128]{1,0:T(8,128)(2,1)S(1)}, bf16[256,128]{1,0:T(8,128)(2,1)}, u32[]{:S(2)}) copy-start(bf16[256,128]{1,0:T(8,128)(2,1)} %copy-done.20) | copy-start | bytes 196612
  113.3 5.0 %copy-start.23 = (bf16[256,512]{1,0:T(8,128)(2,1)S(1)}, bf16[256,512]{1,0:T(8,128)(2,1)}, u32[]{:S(2)}) copy-start(bf16[256,512]{1,0:T(8,128)(2,1)} %copy-done.22) | copy-start | bytes 786436
  116.7 26.5 %copy-start.13 = (f32[1,1024,128]{2,1,0:T(8,128)S(1)}, f32[1,1024,128]{2,1,0:T(8,128)}, u32[]{:S(2)}) copy-start(f32[1,1024,128]{2,1,0:T(8,128)} %copy-done.12) | copy-start | bytes 1572868
  116.7 26.5 %copy-start.25 = (bf16[1,1024,128]{2,1,0:T(8,128)(2,1)S(1)}, bf16[1,1024,128]{2,1,0:T(8,128)(2,1)}, u32[]{:S(2)}) copy-start(bf16[1,1024,128]{2,1,0:T(8,128)(2,1)} %copy-done.24) | copy-start | bytes 786436
  116.7 50.5 %collective-permute-start.6 = (bf16[128,2048]{1,0:T(8,128)(2,1)S(1)}, bf16[128,2048]{1,0:T(8,128)(2,1)S(1)}, u32[]{:S(2)}, u32[]{:S(2)}) collective-permute-start(bf16[128,2048]{1,0:T(8,128)(2,1)S(1)} %project.2), channel_id=1, source_target_pairs={{0,2},{1,3},{2,0},{3,1},{4,6},{5,7},{6,4},{7,5},{8,10},{9,11},{10,... | collective-permute-start | bytes 1572872 | tf_op jit(solution)/shard_map/ppermute | solution.py:404
  162.5 1.4 collective-permute-start.5
  168.1 18.5 %all-to-all-start.2 = ((bf16[8,16,2048]{2,1,0:T(8,128)(2,1)}), bf16[8,16,2048]{2,1,0:T(8,128)(2,1)S(1)}, u32[]{:S(2)}, u32[]{:S(2)}) async-start(bf16[8,16,2048]{2,1,0:T(8,128)(2,1)} %bitcast.11), calls=%async_computation.2 | async-start | bytes 1048576 | tf_op jit(solution)/shard_map/all_to_all | solution.py:411
  171.6 34.7 %copy-start.35 = (bf16[1,128,2048]{2,1,0:T(8,128)(2,1)S(1)}, bf16[1,128,2048]{2,1,0:T(8,128)(2,1)}, u32[]{:S(2)}) copy-start(bf16[1,128,2048]{2,1,0:T(8,128)(2,1)} %param.14) | copy-start | bytes 1572868
  188.0 18.3 %all-to-all-start.3 = ((bf16[8,16,2048]{2,1,0:T(8,128)(2,1)}), bf16[8,16,2048]{2,1,0:T(8,128)(2,1)S(1)}, u32[]{:S(2)}, u32[]{:S(2)}) async-start(bf16[8,16,2048]{2,1,0:T(8,128)(2,1)} %pick.1), calls=%async_computation.3 | async-start | bytes 1048576 | tf_op jit(solution)/shard_map/all_to_all | solution.py:411
  (7 other events, 4.2 us)

commit v4 on v3

--- a/solution.py
+++ b/solution.py
@@ -98,24 +98,26 @@
 
 
 def qkv_kernel(pieces, *refs):
-    xs, (wq, wk, wv, cosine, sine, q, k, v, x, bq, bk, bv, done) = refs[:pieces], refs[pieces:]
+    xs, refs = refs[:pieces], refs[pieces:]
+    wq, wk, wv, cosine, sine, q, k, v, x, bq, bk, bv, bc, bs, done = refs
     rows = xs[0].shape[0]
     copies = [
         pltpu.make_async_copy(piece, x.at[i * rows : (i + 1) * rows, :], done.at[i])
         for i, piece in enumerate(xs)
     ]
-    for i, (w, buffer) in enumerate(((wk, bk), (wv, bv), (wq, bq))):
+    later = ((cosine, bc), (sine, bs), (wk, bk), (wv, bv), (wq, bq))
+    for i, (w, buffer) in enumerate(later):
         copies.append(pltpu.make_async_copy(w, buffer, done.at[pieces + i]))
     for copy in copies:
         copy.start()
-    c, s = cosine[...], sine[...]
-    for copy in copies[: pieces + 1]:
+    for copy in copies[: pieces + 3]:
         copy.wait()
+    c, s = bc[...], bs[...]
     xv = x[...]
     k[...] = turned(jnp.dot(xv, bk[...], preferred_element_type=F32), c, s).astype(BF16)
-    copies[pieces + 1].wait()
+    copies[pieces + 3].wait()
     v[...] = jnp.dot(xv, bv[...], preferred_element_type=F32).astype(BF16)
-    copies[pieces + 2].wait()
+    copies[pieces + 4].wait()
     for j in range(wq.shape[1] // 256):
         got = jnp.dot(xv, bq[:, j * 256 : (j + 1) * 256], preferred_element_type=F32)
         for t in range(2):
@@ -132,21 +134,23 @@
     return pl.pallas_call(
         functools.partial(qkv_kernel, len(xs)),
         out_shape=(out(width), out(LANES), out(LANES)),
-        in_specs=[any_place] * len(xs) + [raw] * 3 + [VM] * 2,
+        in_specs=[any_place] * len(xs) + [raw] * 5,
         out_specs=(VM,) * 3,
         scratch_shapes=[
             pltpu.VMEM((rows, depth), BF16),
             pltpu.VMEM((depth, width), BF16),
             pltpu.VMEM((depth, LANES), BF16),
             pltpu.VMEM((depth, LANES), BF16),
-            pltpu.SemaphoreType.DMA((len(xs) + 3,)),
+            pltpu.VMEM((rows, LANES), F32),
+            pltpu.VMEM((rows, LANES), F32),
+            pltpu.SemaphoreType.DMA((len(xs) + 5,)),
         ],
         compiler_params=pltpu.CompilerParams(vmem_limit_bytes=16 << 20),
         cost_estimate=pl.CostEstimate(
             flops=2 * rows * depth * (width + 2 * LANES), bytes_accessed=5 << 20, transcendentals=0
         ),
         name="qkv",
-    )(*xs, hbm(wq), hbm(wk), hbm(wv), cosine, sine)
+    )(*xs, hbm(wq), hbm(wk), hbm(wv), hbm(cosine), hbm(sine))
 
 
 KEYS = 1024
@@ -154,12 +158,11 @@
 PARTS = 2
 
 
-def att_kernel(chunks, js, mode, scal, q, ka, va, *refs):
+def att_kernel(chunks, which, js, mode, scal, q, ka, va, *refs):
     refs = list(refs)
     take_refs = lambda count: [refs.pop(0) for _ in range(count)]
     if mode != "cached":
         kn, vn = take_refs(chunks), take_refs(chunks)
-        (col,), row = take_refs(1), take_refs(chunks)
     if mode == "new":
         qa_in, acc_in = take_refs(2)
     if mode == "cached":
@@ -179,7 +182,13 @@
     spans = [slice(g * tokens, (g + 1) * tokens) for g in range(per)]
 
     if mode != "cached":
-        allowed = [jnp.broadcast_to(x[...], (tokens, tokens)) <= col[...] for x in row]
+        owned = tokens // 2
+
+        def position(block, axis):
+            i = lax.broadcasted_iota(jnp.int32, (tokens, tokens), axis)
+            return i + jnp.where(i < owned, scal[1 + 2 * block], scal[2 + 2 * block] - owned)
+
+        allowed = [position(block, 1) <= position(which, 0) for block in range(chunks)]
 
     for n, j in enumerate(js):
         if mode == "cached":
@@ -284,7 +293,7 @@
             o[:, at] = jnp.where(lane < HD, pair[0], pltpu.roll(pair[1], HD, 1)).astype(BF16)
 
 
-def attend(js, mode, scal, q, ka, va, kns=(), vns=(), places=(), began=()):
+def attend(which, js, mode, scal, q, ka, va, kns=(), vns=(), began=()):
     tokens, chunks = q.shape[0], PARTS
     rows = q.shape[1] // HD // 2 * tokens
     keys = {"cached": ka.shape[1], "new": tokens * chunks, "full": ka.shape[1] + tokens * chunks}[mode]
@@ -309,9 +318,9 @@
         out = jax.ShapeDtypeStruct((tokens, q.shape[1] // 2 * len(js)), BF16)
         specs = VM
     return pl.pallas_call(
-        functools.partial(att_kernel, chunks, js, mode),
+        functools.partial(att_kernel, chunks, which, js, mode),
         out_shape=out,
-        in_specs=[SM, VM, cached, cached] + [VM] * (len(kns) + len(vns) + len(places) + len(began)),
+        in_specs=[SM, VM, cached, cached] + [VM] * (len(kns) + len(vns) + len(began)),
         out_specs=specs,
         scratch_shapes=scratch,
         compiler_params=pltpu.CompilerParams(vmem_limit_bytes=32 << 20),
@@ -321,7 +330,7 @@
             transcendentals=rows * len(js) * keys,
         ),
         name="attend_" + mode,
-    )(scal, q, ka, va, *kns, *vns, *places, *began)
+    )(scal, q, ka, va, *kns, *vns, *began)
 
 
 def tables(positions):
@@ -383,7 +392,7 @@
 def project(mine, theirs, w, w_pair, kind):
     rows, depth = mine.shape
     width = w.shape[1]
-    step = 512
+    step = 1024
     return pl.pallas_call(
         project_kernel,
         out_shape=jax.ShapeDtypeStruct((rows, width), kind),
@@ -441,7 +450,8 @@
     ).astype(jnp.int32)
     here, there = place((0, near_bit)), place((far_bit, far_bit + near_bit))
     new_tables = [tables(length.astype(F32) + x.astype(F32)) for x in (here, there)]
-    rows_of = [here[None, :], there[None, :]]
+    bits = (0, near_bit, far_bit, far_bit + near_bit)
+    scal = jnp.stack([length] + [((head ^ bit) * positions_here).astype(jnp.int32) for bit in bits])
     held_cos, held_sin = tables(recompute_index[0].astype(F32))
     w_pair = swap(output_weight, "head", near_bit)
     slots = jnp.arange(slot_request.shape[0], dtype=jnp.int32)
@@ -468,7 +478,7 @@
     near = swap(own, "head", near_bit)
     weights = (query_weight, key_weight, value_weight)
     q_here, kn_here, vn_here = qkv([own, near], *weights, *new_tables[0])
-    began = attend((0,), "cached", cache_lengths, q_here, ka, va)
+    began = attend(0, (0,), "cached", scal, q_here, ka, va)
     far, began = tie((far, began))
     corner = swap(far, "head", near_bit)
     q_there, kn_there, vn_there = qkv([far, corner], *weights, *new_tables[1])
@@ -478,11 +488,11 @@
         theirs = swap(attended[positions_here:], "head", near_bit)
         return project(attended[:positions_here], theirs, output_weight, w_pair, kind)
 
-    args = (cache_lengths, q_there, ka, va, kns, vns, [there[:, None], *rows_of])
-    sent = turn_over(attend((0, 1), "full", *args), BF16)
+    args = (scal, q_there, ka, va, kns, vns)
+    sent = turn_over(attend(1, (0, 1), "full", *args), BF16)
     sent, q_here = tie((sent, q_here))
-    args = (cache_lengths, q_here, ka, va, kns, vns, [here[:, None], *rows_of])
-    halves = [attend((0,), "new", *args, began), attend((1,), "full", *args)]
+    args = (scal, q_here, ka, va, kns, vns)
+    halves = [attend(0, (0,), "new", *args, began), attend(0, (1,), "full", *args)]
     kept = turn_over(jnp.concatenate(halves, axis=1), F32)
     got = swap(sent, "head", far_bit)
     back = spread((kept + got.astype(F32)).astype(BF16))

time: 208 us -> 205 us (0.986)
  Pallas kernels: 120 us -> 80.3 us
  starting transfers between devices: 22.3 us -> 57.7 us
  waiting for transfers between devices: 40.6 us -> 48.2 us
  local copies, waits for them, and re-layouts: 14.9 us -> 7.84 us
    pallas_call x4, Pallas kernels: 99.1 us -> 61.6 us  [attend(): pl.pallas_call(functools.partial(att_kernel, chunks, which, js, mode), ou...]
    all_to_all x4, starting transfers between devices: 18.5 us -> 54.1 us  [spread(): lax.all_to_all(pieces, 'req', split_axis=0, concat_axis=0, tiled=True)]
    ppermute x7, waiting for transfers between devices: 3.67 us -> 10.2 us  [swap(): return lax.ppermute(x, axis, [(i, i ^ bits) for i in range(size)])]
    unnamed x88 -> x28, local copies, waits for them, and re-layouts: 12.8 us -> 6.59 us
    pallas_call x2, Pallas kernels: 6.65 us -> 4.56 us  [project(): pl.pallas_call(project_kernel, out_shape=jax.ShapeDtypeStruct((rows, widt...]
  transfers between devices with their start and end apart: 11 -> 11, of which waited for: 9 -> 9; matrix products, arithmetic and copies ran while one was open for 4% -> 4% of each run, Pallas kernels for 55% -> 37%
where the time goes in v4:
time: 205 us
  Pallas kernels  80.3 us (39%)
  starting transfers between devices  57.7 us (28%)
  waiting for transfers between devices  48.2 us (24%)
  other arithmetic  8.96 us (4%)
  local copies, waits for them, and re-layouts  7.84 us (4%)
    pallas_call x4, Pallas kernels, attend(): pl.pallas_call(functools.partial(att_kernel, chunks, which, js, mode), ou...  61.6 us
    all_to_all x4, starting transfers between devices, spread(): lax.all_to_all(pieces, 'req', split_axis=0, concat_axis=0, tiled=True)  54.1 us
    all_to_all x4, waiting for transfers between devices, spread(): lax.all_to_all(pieces, 'req', split_axis=0, concat_axis=0, tiled=True)  38 us
    ppermute x7, waiting for transfers between devices, swap(): return lax.ppermute(x, axis, [(i, i ^ bits) for i in range(size)])  10.2 us
    pallas_call x2, Pallas kernels, qkv(): pl.pallas_call(functools.partial(qkv_kernel, len(xs)), out_shape=(out(wid...  6.61 us
    unnamed x28, local copies, waits for them, and re-layouts  6.59 us
    pallas_call x1, Pallas kernels, prep(): pl.pallas_call(prep_kernel, out_shape=(out, out), in_specs=[SM] + [VM] *...  4.58 us
    pallas_call x2, Pallas kernels, project(): pl.pallas_call(project_kernel, out_shape=jax.ShapeDtypeStruct((rows, widt...  4.56 us
  transfers between devices with their start and end apart: 11, of which 9 were waited for; matrix products, arithmetic and copies ran while one was open for 4% of the time, Pallas kernels for 37%

profile of v4, /device:TPU:0, one launch (start us, length us, event | category | flops | bytes accessed | tf_op | source)
XLA Modules:
  0.0 204.6 jit_solution(11832688653130001961)
XLA Ops:
  0.6 7.3 %all-to-all-start = ((bf16[8,16,2048]{2,1,0:T(8,128)(2,1)}), bf16[8,16,2048]{2,1,0:T(8,128)(2,1)S(1)}, u32[]{:S(2)}, u32[]{:S(2)}) async-start(bf16[8,16,2048]{2,1,0:T(8,128)(2,1)} %bitcast.25), calls=%async_computation | async-start | bytes 1048576 | tf_op jit(solution)/shard_map/all_to_all | solution.py:420
  8.7 1.0 fusion.4
  9.7 0.7 convert_reduce_fusion
  10.4 0.8 pad_maximum_fusion.3.refs_5_
  11.2 0.8 pad_maximum_fusion.5.refs_5_
  12.0 0.8 pad_maximum_fusion.4.refs_6_
  12.8 0.8 pad_maximum_fusion.6.refs_6_
  13.7 0.8 fusion.2
  14.4 0.4 pad_maximum_fusion
  14.8 7.6 %all-to-all-done.x = bf16[8,16,2048]{2,1,0:T(8,128)(2,1)S(1)} async-done(((bf16[8,16,2048]{2,1,0:T(8,128)(2,1)}), bf16[8,16,2048]{2,1,0:T(8,128)(2,1)S(1)}, u32[]{:S(2)}, u32[]{:S(2)}) %all-to-all-start) | async-done | bytes 524320 | tf_op jit(solution)/shard_map/all_to_all | solution.py:420
  22.4 1.6 pick_norm.1
  23.9 4.2 %all-to-all-start.1 = ((bf16[8,16,2048]{2,1,0:T(8,128)(2,1)}), bf16[8,16,2048]{2,1,0:T(8,128)(2,1)}, u32[]{:S(2)}, u32[]{:S(2)}) async-start(bf16[8,16,2048]{2,1,0:T(8,128)(2,1)} %pick_norm.1), calls=%async_computation.1 | async-start | bytes 1048576 | tf_op jit(solution)/shard_map/all_to_all | solution.py:420
  28.2 1.4 copy-done.10
  29.6 1.2 copy-done.11
  30.8 1.2 copy-done.12
  32.0 4.6 %prep.1 = (bf16[2,4096,128]{2,1,0:T(8,128)(2,1)S(1)}, bf16[2,4096,128]{2,1,0:T(8,128)(2,1)S(1)}) custom-call(s32[1]{0:T(128)S(6)} %copy.18.length, bf16[384,2048]{1,0:T(8,128)(2,1)S(1)} %bitcast.22, f32[1,2048]{1,0:T(1,128)S(1)} %bitcast.21, bf16[2048,128]{1,0:T(8,128)(2,1)S(1)} %copy-done.5, bf16[2048,128]{1,0:T(8,128)(2,1)S(1)} %copy-done.6, ...), custom_call_target="tpu_custom_call" | custom-call | flops 3000000000 | bytes 8388608 | tf_op jit(solution)/shard_map/prep/pallas_call | solution.py:88
  36.6 1.3 copy-done.1
  37.9 1.4 copy-done.3
  39.3 3.1 %all-to-all-done.1 = bf16[8,16,2048]{2,1,0:T(8,128)(2,1)} async-done(((bf16[8,16,2048]{2,1,0:T(8,128)(2,1)}), bf16[8,16,2048]{2,1,0:T(8,128)(2,1)}, u32[]{:S(2)}, u32[]{:S(2)}) %all-to-all-start.1) | async-done | bytes 524320 | tf_op jit(solution)/shard_map/all_to_all | solution.py:420
  42.4 1.5 collective-permute-start
  43.9 0.2 collective-permute-start.4
  44.2 0.1 stack.19.scal
  44.2 0.3 collective-permute-done.1.refs_1_
  44.5 3.4 %qkv.2 = (bf16[256,512]{1,0:T(8,128)(2,1)S(1)}, bf16[256,128]{1,0:T(8,128)(2,1)S(1)}, bf16[256,128]{1,0:T(8,128)(2,1)S(1)}) custom-call(bf16[128,2048]{1,0:T(8,128)(2,1)} %bitcast.7.refs_0_, bf16[128,2048]{1,0:T(8,128)(2,1)S(1)} %collective-permute-done.1.refs_1_, bf16[2048,512]{1,0:T(8,128)(2,1)} %refs_2_.3, bf16[2048,128]{1,0:T(8,128)(2,1)} %refs_3_.3, ...), custom_call_target="tpu_custom_call" | custom-call | flops 805306368 | bytes 5242880 | tf_op jit(solution)/shard_map/qkv/pallas_call | solution.py:134
  47.9 3.5 %attend_cached.1 = (bf16[1,1024,128]{2,1,0:T(8,128)(2,1)S(1)}, f32[1,1024,128]{2,1,0:T(8,128)S(1)}) custom-call(s32[5]{0:T(128)S(1)} %stack.19.scal, bf16[256,512]{1,0:T(8,128)(2,1)S(1)} %get-tuple-element.50.q, bf16[2,4096,128]{2,1,0:T(8,128)(2,1)S(1)} %copy-done.2, bf16[2,4096,128]{2,1,0:T(8,128)(2,1)S(1)} %copy-done.4), custom_call_target="tpu_custom_call" | custom-call | flops 4294967296 | bytes 4194304 | tf_op jit(solution)/shard_map/attend_cached/pallas_call | solution.py:320
  51.5 5.5 %collective-permute-done.refs_0_ = bf16[128,2048]{1,0:T(8,128)(2,1)S(1)} collective-permute-done((bf16[128,2048]{1,0:T(8,128)(2,1)}, bf16[128,2048]{1,0:T(8,128)(2,1)S(1)}, u32[]{:S(2)}, u32[]{:S(2)}) %collective-permute-start) | collective-permute-done | bytes 524320 | tf_op jit(solution)/shard_map/ppermute | solution.py:413
  57.0 1.9 collective-permute-done.2.refs_1_
  58.9 3.2 %qkv.3 = (bf16[256,512]{1,0:T(8,128)(2,1)S(1)}, bf16[256,128]{1,0:T(8,128)(2,1)S(1)}, bf16[256,128]{1,0:T(8,128)(2,1)S(1)}) custom-call(bf16[128,2048]{1,0:T(8,128)(2,1)S(1)} %collective-permute-done.refs_0_, bf16[128,2048]{1,0:T(8,128)(2,1)S(1)} %collective-permute-done.2.refs_1_, bf16[2048,512]{1,0:T(8,128)(2,1)} %refs_2_.3, bf16[2048,128]{1,0:T(8,128)(2,1)} %refs_3_.3, ...), custom_call_target="tpu_custom_call" | custom-call | flops 805306368 | bytes 5242880 | tf_op jit(solution)/shard_map/qkv/pallas_call | solution.py:134
  62.1 30.2 %attend_full.2 = bf16[256,512]{1,0:T(8,128)(2,1)S(1)} custom-call(s32[5]{0:T(128)S(1)} %stack.19.scal, bf16[256,512]{1,0:T(8,128)(2,1)S(1)} %get-tuple-element.45.q, bf16[2,4096,128]{2,1,0:T(8,128)(2,1)S(1)} %copy-done.2, bf16[2,4096,128]{2,1,0:T(8,128)(2,1)S(1)} %copy-done.4, bf16[256,128]{1,0:T(8,128)(2,1)S(1)} %get-tuple-element.46.refs_0_, ...), custom_call_target="tpu_custom_call" | custom-call | flops 9663676416 | bytes 4194304 | tf_op jit(solution)/shard_map/attend_full/pallas_call | solution.py:320
  92.3 0.2 collective-permute-start.3
  92.5 1.2 collective-permute-done.3.theirs
  93.7 2.3 %project.2 = bf16[128,2048]{1,0:T(8,128)(2,1)S(1)} custom-call(bf16[128,512]{1,0:T(8,128)(2,1)S(1)} %get-tuple-element.57.mine, bf16[128,512]{1,0:T(8,128)(2,1)S(1)} %collective-permute-done.3.theirs, bf16[512,2048]{1,0:T(8,128)(2,1)S(1)} %copy-done, bf16[512,2048]{1,0:T(8,128)(2,1)} %collective-permute-done.4.w_pair), custom_call_target="tpu_custom_call" | custom-call | flops 536870912 | bytes 6291456 | tf_op jit(solution)/shard_map/project/pallas_call | solution.py:396
  96.0 1.6 collective-permute-start.6
  97.6 15.4 %attend_full.3 = bf16[256,256]{1,0:T(8,128)(2,1)S(1)} custom-call(s32[5]{0:T(128)S(1)} %stack.19.scal, bf16[256,512]{1,0:T(8,128)(2,1)S(1)} %get-tuple-element.50.q, bf16[2,4096,128]{2,1,0:T(8,128)(2,1)S(1)} %copy-done.2, bf16[2,4096,128]{2,1,0:T(8,128)(2,1)S(1)} %copy-done.4, bf16[256,128]{1,0:T(8,128)(2,1)S(1)} %get-tuple-element.46.refs_0_, ...), custom_call_target="tpu_custom_call" | custom-call | flops 4831838208 | bytes 4194304 | tf_op jit(solution)/shard_map/attend_full/pallas_call | solution.py:320
  113.0 12.4 %attend_new.1 = bf16[256,256]{1,0:T(8,128)(2,1)S(1)} custom-call(s32[5]{0:T(128)S(1)} %stack.19.scal, bf16[256,512]{1,0:T(8,128)(2,1)S(1)} %get-tuple-element.50.q, bf16[2,4096,128]{2,1,0:T(8,128)(2,1)S(1)} %copy-done.2, bf16[2,4096,128]{2,1,0:T(8,128)(2,1)S(1)} %copy-done.4, bf16[256,128]{1,0:T(8,128)(2,1)S(1)} %get-tuple-element.46.refs_0_, ...), custom_call_target="tpu_custom_call" | custom-call | flops 536870912 | bytes 4194304 | tf_op jit(solution)/shard_map/attend_new/pallas_call | solution.py:320
  125.6 1.3 collective-permute-done.5.theirs
  126.9 2.3 %project.3 = f32[128,2048]{1,0:T(8,128)S(1)} custom-call(bf16[128,512]{1,0:T(8,128)(2,1)S(1)} %get-tuple-element.55.mine, bf16[128,512]{1,0:T(8,128)(2,1)S(1)} %collective-permute-done.5.theirs, bf16[512,2048]{1,0:T(8,128)(2,1)S(1)} %copy-done, bf16[512,2048]{1,0:T(8,128)(2,1)} %collective-permute-done.4.w_pair), custom_call_target="tpu_custom_call" | custom-call | flops 536870912 | bytes 6291456 | tf_op jit(solution)/shard_map/project/pallas_call | solution.py:396
  129.2 0.9 add_convert_fusion
  130.1 39.0 %all-to-all-start.2 = ((bf16[8,16,2048]{2,1,0:T(8,128)(2,1)}), bf16[8,16,2048]{2,1,0:T(8,128)(2,1)S(1)}, u32[]{:S(2)}, u32[]{:S(2)}) async-start(bf16[8,16,2048]{2,1,0:T(8,128)(2,1)} %bitcast.11), calls=%async_computation.2 | async-start | bytes 1048576 | tf_op jit(solution)/shard_map/all_to_all | solution.py:420
  169.1 0.1 select_reduce_fusion.order
  169.2 14.7 %all-to-all-done.2.x = bf16[8,16,2048]{2,1,0:T(8,128)(2,1)S(1)} async-done(((bf16[8,16,2048]{2,1,0:T(8,128)(2,1)}), bf16[8,16,2048]{2,1,0:T(8,128)(2,1)S(1)}, u32[]{:S(2)}, u32[]{:S(2)}) %all-to-all-start.2) | async-done | bytes 524320 | tf_op jit(solution)/shard_map/all_to_all | solution.py:420
  183.9 1.4 pick.1
  185.3 3.6 %all-to-all-start.3 = ((bf16[8,16,2048]{2,1,0:T(8,128)(2,1)}), bf16[8,16,2048]{2,1,0:T(8,128)(2,1)S(1)}, u32[]{:S(2)}, u32[]{:S(2)}) async-start(bf16[8,16,2048]{2,1,0:T(8,128)(2,1)} %pick.1), calls=%async_computation.3 | async-start | bytes 1048576 | tf_op jit(solution)/shard_map/all_to_all | solution.py:420
  189.0 0.6 gather_fusion.1
  189.6 0.6 gather_fusion
  190.2 0.8 broadcast_select_fusion
  191.0 12.6 %all-to-all-done.3 = bf16[8,16,2048]{2,1,0:T(8,128)(2,1)S(1)} async-done(((bf16[8,16,2048]{2,1,0:T(8,128)(2,1)}), bf16[8,16,2048]{2,1,0:T(8,128)(2,1)S(1)}, u32[]{:S(2)}, u32[]{:S(2)}) %all-to-all-start.3) | async-done | bytes 524320 | tf_op jit(solution)/shard_map/all_to_all | solution.py:420
  203.6 0.9 fusion
  (41 shorter events, 0.2 us)
Async XLA Ops:
  0.6 21.8 %all-to-all-start = ((bf16[8,16,2048]{2,1,0:T(8,128)(2,1)}), bf16[8,16,2048]{2,1,0:T(8,128)(2,1)S(1)}, u32[]{:S(2)}, u32[]{:S(2)}) async-start(bf16[8,16,2048]{2,1,0:T(8,128)(2,1)} %bitcast.25), calls=%async_computation | async-start | bytes 1048576 | tf_op jit(solution)/shard_map/all_to_all | solution.py:420
  7.9 14.5 %copy-start.7 = (f32[2048]{0:T(1024)S(1)}, f32[2048]{0:T(1024)}, u32[]{:S(2)}) copy-start(f32[2048]{0:T(1024)} %param.15) | copy-start | bytes 24580
  7.9 14.5 %copy-start.9 = (s32[8]{0:T(128)S(1)}, s32[8]{0:T(128)}, u32[]{:S(2)}) copy-start(s32[8]{0:T(128)} %order.1) | copy-start | bytes 100
  12.8 15.3 %copy-start.5 = (bf16[2048,128]{1,0:T(8,128)(2,1)S(1)}, bf16[2048,128]{1,0:T(8,128)(2,1)}, u32[]{:S(2)}) copy-start(bf16[2048,128]{1,0:T(8,128)(2,1)} %refs_3_.3) | copy-start | bytes 1572868
  12.8 15.3 %copy-start.6 = (bf16[2048,128]{1,0:T(8,128)(2,1)S(1)}, bf16[2048,128]{1,0:T(8,128)(2,1)}, u32[]{:S(2)}) copy-start(bf16[2048,128]{1,0:T(8,128)(2,1)} %refs_4_.3) | copy-start | bytes 1572868
  12.8 15.3 %copy-start.8 = (s32[1,384]{1,0:T(1,128)S(1)}, s32[1,384]{1,0:T(1,128)}, u32[]{:S(2)}) copy-start(s32[1,384]{1,0:T(1,128)} %index.1) | copy-start | bytes 4612
  23.9 18.5 %all-to-all-start.1 = ((bf16[8,16,2048]{2,1,0:T(8,128)(2,1)}), bf16[8,16,2048]{2,1,0:T(8,128)(2,1)}, u32[]{:S(2)}, u32[]{:S(2)}) async-start(bf16[8,16,2048]{2,1,0:T(8,128)(2,1)} %pick_norm.1), calls=%async_computation.1 | async-start | bytes 1048576 | tf_op jit(solution)/shard_map/all_to_all | solution.py:420
  28.1 1.4 copy-start.10
  29.6 1.2 copy-start.11
  30.8 1.2 copy-start.12
  32.0 11.9 %copy-start = (bf16[512,2048]{1,0:T(8,128)(2,1)S(1)}, bf16[512,2048]{1,0:T(8,128)(2,1)}, u32[]{:S(2)}) copy-start(bf16[512,2048]{1,0:T(8,128)(2,1)} %w.3) | copy-start | bytes 6291460
  36.6 1.3 copy-start.1
  37.9 1.4 copy-start.3
  42.4 2.1 %collective-permute-start.1 = (bf16[128,2048]{1,0:T(8,128)(2,1)}, bf16[128,2048]{1,0:T(8,128)(2,1)S(1)}, u32[]{:S(2)}, u32[]{:S(2)}) collective-permute-start(bf16[128,2048]{1,0:T(8,128)(2,1)} %bitcast.7.refs_0_), channel_id=1, source_target_pairs={{0,1},{1,0},{2,3},{3,2},{4,5},{5,4},{6,7},{7,6},{8,9},{9,8},{10,11... | collective-permute-start | bytes 1572872 | tf_op jit(solution)/shard_map/ppermute | solution.py:413
  42.4 14.5 %collective-permute-start = (bf16[128,2048]{1,0:T(8,128)(2,1)}, bf16[128,2048]{1,0:T(8,128)(2,1)S(1)}, u32[]{:S(2)}, u32[]{:S(2)}) collective-permute-start(bf16[128,2048]{1,0:T(8,128)(2,1)} %bitcast.7.refs_0_), channel_id=1, source_target_pairs={{0,2},{1,3},{2,0},{3,1},{4,6},{5,7},{6,4},{7,5},{8,10},{9,11},{10,... | collective-permute-start | bytes 1572872 | tf_op jit(solution)/shard_map/ppermute | solution.py:413
  43.9 48.6 %collective-permute-start.4 = (bf16[512,2048]{1,0:T(8,128)(2,1)S(1)}, bf16[512,2048]{1,0:T(8,128)(2,1)}, u32[]{:S(2)}, u32[]{:S(2)}) collective-permute-start(bf16[512,2048]{1,0:T(8,128)(2,1)S(1)} %copy-done), channel_id=1, source_target_pairs={{0,1},{1,0},{2,3},{3,2},{4,5},{5,4},{6,7},{7,6},{8,9},{9,8},{10,11... | collective-permute-start | bytes 6291464 | tf_op jit(solution)/shard_map/ppermute | solution.py:413
  44.2 3.7 %copy-start.2 = (bf16[2,4096,128]{2,1,0:T(8,128)(2,1)S(1)}, bf16[2,4096,128]{2,1,0:T(8,128)(2,1)}, u32[]{:S(2)}) copy-start(bf16[2,4096,128]{2,1,0:T(8,128)(2,1)} %copy-done.1) | copy-start | bytes 6291460
  44.2 3.7 %copy-start.4 = (bf16[2,4096,128]{2,1,0:T(8,128)(2,1)S(1)}, bf16[2,4096,128]{2,1,0:T(8,128)(2,1)}, u32[]{:S(2)}) copy-start(bf16[2,4096,128]{2,1,0:T(8,128)(2,1)} %copy-done.3) | copy-start | bytes 6291460
  57.0 1.9 collective-permute-start.2
  92.3 1.4 collective-permute-start.3
  96.0 33.2 %collective-permute-start.6 = (bf16[128,2048]{1,0:T(8,128)(2,1)S(1)}, bf16[128,2048]{1,0:T(8,128)(2,1)S(1)}, u32[]{:S(2)}, u32[]{:S(2)}) collective-permute-start(bf16[128,2048]{1,0:T(8,128)(2,1)S(1)} %project.2), channel_id=1, source_target_pairs={{0,2},{1,3},{2,0},{3,1},{4,6},{5,7},{6,4},{7,5},{8,10},{9,11},{10,... | collective-permute-start | bytes 1572872 | tf_op jit(solution)/shard_map/ppermute | solution.py:413
  125.5 1.4 collective-permute-start.5
  130.1 53.8 %all-to-all-start.2 = ((bf16[8,16,2048]{2,1,0:T(8,128)(2,1)}), bf16[8,16,2048]{2,1,0:T(8,128)(2,1)S(1)}, u32[]{:S(2)}, u32[]{:S(2)}) async-start(bf16[8,16,2048]{2,1,0:T(8,128)(2,1)} %bitcast.11), calls=%async_computation.2 | async-start | bytes 1048576 | tf_op jit(solution)/shard_map/all_to_all | solution.py:420
  169.1 34.5 %copy-start.13 = (bf16[1,128,2048]{2,1,0:T(8,128)(2,1)S(1)}, bf16[1,128,2048]{2,1,0:T(8,128)(2,1)}, u32[]{:S(2)}) copy-start(bf16[1,128,2048]{2,1,0:T(8,128)(2,1)} %param.14) | copy-start | bytes 1572868
  185.3 18.3 %all-to-all-start.3 = ((bf16[8,16,2048]{2,1,0:T(8,128)(2,1)}), bf16[8,16,2048]{2,1,0:T(8,128)(2,1)S(1)}, u32[]{:S(2)}, u32[]{:S(2)}) async-start(bf16[8,16,2048]{2,1,0:T(8,128)(2,1)} %pick.1), calls=%async_computation.3 | async-start | bytes 1048576 | tf_op jit(solution)/shard_map/all_to_all | solution.py:420
